TPU v7x, 128 devices: a whole 4x4x4 slice. The times are simulated.
128 devices in a mesh: gx: 8 (over y, z_lo), gy: 16 (over x, z_hi, core).
Axes of the slice: x: 4, y: 4, z: 4 (z_hi: 2, z_lo: 2; z = z_hi * 2 + z_lo), core: 2. Of those that a mesh axis runs over, the one named last changes fastest.
Arguments:
- selectors: float32 [3, 8, 8, 16, 65536], P(None, None, 'gx', 'gy'), may hold values from 0 to 2047, as said below
- proofs: float32 [3, 8, 8, 16, 65536], P(None, None, 'gx', 'gy'), may hold values from 0 to 2047, as said below
- challenges: int32 [4], replicated, may hold values from 0 to 2147483646
Outputs:
- round_values: float32 [3, 4, 3], replicated
- folded_selectors: float32 [3, 8, 8, 16, 4096], P(None, None, 'gx', 'gy')
- folded_proofs: float32 [3, 8, 8, 16, 4096], P(None, None, 'gx', 'gy')
Inputs may be any that keep to these rules, and one draw needn't show every extreme that they name: `selectors`: limbs of field elements, as in the first step. `proofs`: limbs of field elements, as in the first step. `challenges`: field elements.
All inputs are finite; a program needn't handle non-finite values.
Results may differ from a plain program's by a relative error of at most 0.0003.
Values sent between devices are 32-bit elements; how exact they have to be, the bound alone decides.
A program may use at most 128 MiB of HBM per device.

v0:
```python
import jax
import jax.numpy as jnp
from jax import lax
from jax.sharding import PartitionSpec as P


def from_partner(x, axis, stride):
    return lax.ppermute(x, axis, [(i, i ^ 1 << stride) for i in range(lax.axis_size(axis))])


def settle(lowest, middle, highest):
    for repeat in range(3):
        carried = jnp.floor(lowest / 2048.0)
        lowest = lowest - carried * 2048.0
        middle = middle + carried
        carried = jnp.floor(middle / 2048.0)
        middle = middle - carried * 2048.0
        highest = highest + carried
        carried = jnp.floor(highest / 512.0)
        highest = highest - carried * 512.0
        lowest = lowest + carried
    at_modulus = (lowest == 2047.0) & (middle == 2047.0) & (highest == 511.0)
    nothing = jnp.zeros_like(lowest)
    return jnp.stack(
        [
            jnp.where(at_modulus, nothing, lowest),
            jnp.where(at_modulus, nothing, middle),
            jnp.where(at_modulus, nothing, highest),
        ]
    )


def field_add(augend, addend):
    return settle(augend[0] + addend[0], augend[1] + addend[1], augend[2] + addend[2])


def field_sub(minuend, subtrahend):
    return settle(
        minuend[0] + 2047.0 - subtrahend[0],
        minuend[1] + 2047.0 - subtrahend[1],
        minuend[2] + 511.0 - subtrahend[2],
    )


def field_mul(factor, multiplier):
    degree_zero = factor[0] * multiplier[0]
    degree_one = factor[0] * multiplier[1] + factor[1] * multiplier[0]
    degree_two = factor[0] * multiplier[2] + factor[1] * multiplier[1] + factor[2] * multiplier[0]
    degree_three = factor[1] * multiplier[2] + factor[2] * multiplier[1]
    degree_four = factor[2] * multiplier[2]
    carried = jnp.floor(degree_zero / 2048.0)
    degree_zero = degree_zero - carried * 2048.0
    degree_one = degree_one + carried
    carried = jnp.floor(degree_one / 2048.0)
    degree_one = degree_one - carried * 2048.0
    degree_two = degree_two + carried
    carried = jnp.floor(degree_two / 2048.0)
    degree_two = degree_two - carried * 2048.0
    degree_three = degree_three + carried
    carried = jnp.floor(degree_three / 2048.0)
    degree_three = degree_three - carried * 2048.0
    degree_four = degree_four + carried
    return settle(degree_zero + 4.0 * degree_three, degree_one + 4.0 * degree_four, degree_two)


def field_sum(values):
    values = values.reshape(3, -1)
    length = values.shape[1]
    while length > 1:
        stride = min(length, 2048)
        summed = values.reshape(3, length // stride, stride).sum(axis=2)
        values = settle(summed[0], summed[1], summed[2])
        length = length // stride
    return values.reshape(3)


def round_points(select_low, select_high, proof_low, proof_high):
    at_zero = field_sum(field_mul(select_low, proof_low))
    at_one = field_sum(field_mul(select_high, proof_high))
    select_two = field_sub(field_add(select_high, select_high), select_low)
    proof_two = field_sub(field_add(proof_high, proof_high), proof_low)
    at_two = field_sum(field_mul(select_two, proof_two))
    return jnp.stack([at_zero, at_one, at_two], axis=1)


def fold_tables(low_table, high_table, scalar):
    scalar = scalar.reshape((3,) + (1,) * (low_table.ndim - 1))
    return field_add(low_table, field_mul(field_sub(high_table, low_table), scalar))


def challenge_limbs(challenges, position):
    element = challenges[position]
    return jnp.stack([element & 2047, element >> 11 & 2047, element >> 22]).astype(jnp.float32)


def pack_words(limbs):
    return jnp.stack([limbs[0] + 2048.0 * limbs[1], limbs[2]])


def unpack_words(words):
    upper = jnp.floor(words[0] / 2048.0)
    return jnp.stack([words[0] - upper * 2048.0, upper, words[1]])


def halves(tables, own_bit, sender):
    half_rows = tables[0].shape[-1] // 2
    kept_parts = tuple(
        (
            lax.dynamic_slice_in_dim(one_table, own_bit * half_rows, half_rows, 2)
            for one_table in tables
        )
    )
    given_parts = tuple(
        (
            pack_words(lax.dynamic_slice_in_dim(one_table, (1 - own_bit) * half_rows, half_rows, 2))
            for one_table in tables
        )
    )
    received = tuple((unpack_words(got_one) for got_one in sender(given_parts)))
    is_low = own_bit == 0
    lower_part = tuple(
        (jnp.where(is_low, kept_one, got_one) for kept_one, got_one in zip(kept_parts, received))
    )
    upper_part = tuple(
        (jnp.where(is_low, got_one, kept_one) for kept_one, got_one in zip(kept_parts, received))
    )
    return (lower_part, upper_part)


def publish(points):
    summed = lax.psum(points, ("gx", "gy"))
    return settle(summed[0], summed[1], summed[2])


def bind_pair(select_table, proof_table, first_scalar, second_scalar, on_first):
    if on_first:
        device_index = lax.axis_index("gx")
        bit_count = lax.axis_size("gx").bit_length() - 1
    else:
        device_index = lax.axis_index("gy")
        bit_count = lax.axis_size("gy").bit_length() - 1
    top_position = bit_count - 1
    low_position = bit_count - 2
    top_bit = device_index >> top_position & 1
    low_bit = device_index >> low_position & 1

    def top_sender(given_parts):
        if on_first:
            return from_partner((given_parts[0], given_parts[1]), "gx", top_position)
        return from_partner((given_parts[0], given_parts[1]), "gy", top_position)

    def folded_sender(given_parts):
        if on_first:
            return from_partner((given_parts[0], given_parts[1]), "gx", low_position)
        return from_partner((given_parts[0], given_parts[1]), "gy", low_position)

    lower_part, upper_part = halves((select_table, proof_table), top_bit, top_sender)
    select_low, proof_low = lower_part
    select_high, proof_high = upper_part
    first_points = publish(round_points(select_low, select_high, proof_low, proof_high))
    select_table = fold_tables(select_low, select_high, first_scalar)
    proof_table = fold_tables(proof_low, proof_high, first_scalar)
    lower_part, upper_part = halves((select_table, proof_table), low_bit, folded_sender)
    second_points = publish(
        round_points(lower_part[0], upper_part[0], lower_part[1], upper_part[1])
    )
    select_table = fold_tables(lower_part[0], upper_part[0], second_scalar)
    proof_table = fold_tables(lower_part[1], upper_part[1], second_scalar)
    return (select_table, proof_table, first_points, second_points)


def shards(selectors, proofs, challenges):
    row_count = selectors.shape[-1]
    polynomials = selectors.shape[1]
    select_table = selectors.reshape(3, polynomials, row_count)
    proof_table = proofs.reshape(3, polynomials, row_count)
    scalars = [challenge_limbs(challenges, position) for position in range(4)]
    select_table, proof_table, first_points, second_points = bind_pair(
        select_table, proof_table, scalars[0], scalars[1], True
    )
    select_table, proof_table, third_points, fourth_points = bind_pair(
        select_table, proof_table, scalars[2], scalars[3], False
    )
    stacked = jnp.stack([first_points, second_points, third_points, fourth_points], axis=1)
    final_rows = row_count // 16
    return (
        stacked,
        select_table.reshape(3, polynomials, 1, 1, final_rows),
        proof_table.reshape(3, polynomials, 1, 1, final_rows),
    )


def solution(mesh):
    in_specs = (P(None, None, "gx", "gy", None), P(None, None, "gx", "gy", None), P())
    out_specs = (P(), P(None, None, "gx", "gy", None), P(None, None, "gx", "gy", None))
    return jax.shard_map(shards, mesh=mesh, in_specs=in_specs, out_specs=out_specs, check_vma=False)
```

profile of v0, /device:TPU:1, one launch (start us, length us, event | category | flops | bytes accessed | tf_op | source)
XLA Modules:
  0.0 482.6 jit_solution(14959047600122539789)
XLA Ops:
  0.6 3.1 constant_dynamic-slice_fusion.1
  7.1 3.7 collective-permute-start
  25.3 2.1 constant_dynamic-slice_fusion.13
  27.4 2.1 constant_dynamic-slice_fusion.11
  29.5 26.7 %collective-permute-done = f32[2,8,32768]{2,1,0:T(8,128)} collective-permute-done((f32[2,8,32768]{2,1,0:T(8,128)}, f32[2,8,32768]{2,1,0:T(8,128)}, u32[]{:S(2)}, u32[]{:S(2)}) %collective-permute-start) | collective-permute-done | bytes 2097184 | tf_op jit(solution)/shard_map/ppermute | solution.py:8
  56.2 1.7 multiply_subtract_fusion.27
  57.9 3.7 bitcast_select_fusion.2
  61.6 39.5 %collective-permute-done.1 = f32[2,8,32768]{2,1,0:T(8,128)} collective-permute-done((f32[2,8,32768]{2,1,0:T(8,128)}, f32[2,8,32768]{2,1,0:T(8,128)}, u32[]{:S(2)}, u32[]{:S(2)}) %collective-permute-start.1) | collective-permute-done | bytes 2097184 | tf_op jit(solution)/shard_map/ppermute | solution.py:8
  101.1 1.7 multiply_subtract_fusion.26
  102.9 1.9 bitcast_select_fusion
  104.8 6.1 %broadcast_select_fusion.3 = (f32[1,8,32768]{2,1,0:T(8,128)}, pred[1,8,32768]{2,1,0:T(8,128)(4,1)S(1)}, f32[1,8,32768]{2,1,0:T(8,128)}, f32[1,8,32768]{2,1,0:T(8...) fusion(f32[3,8,32768]{2,1,0:T(8,128)S(1)} %get-tuple-element.33, ...), kind=kLoop, calls=%fused_computation.705 | loop fusion | flops 35651584 | bytes 14942208 | tf_op jit(solution)/shard_map/jit(_where)/select_n | solution.py:26
  110.9 2.4 stack.568
  113.3 4.7 fusion.94
  118.0 2.4 stack.569
  120.4 2.4 stack.570
  122.8 2.2 maximum_reduce_fusion.1
  128.5 10.1 %fusion.69 = (f32[1,8,32768]{2,1,0:T(8,128)S(1)}, f32[1,8,32768]{2,1,0:T(8,128)S(1)}, f32[1,8,32768]{2,1,0:T(8,128)S(1)}, f32[1,8,32768]{2,1,0:T(8,128)}, f32[1,8,32768]{2,1,0:T(8,128)}, /*index=5*/f32[1,8,32768]{2,1,0:T(8,128)}) fusion(f32[3,8,32768]{2,1,0:T(8,128)S(1)} %copy-done, f32[1,8,32768]{2,1,0:T(8,128)} %get-tuple-element.366, ...), kind=kLoop, calls=%fused_computation.260 | loop fusion | flops 43253760 | bytes 14680076 | tf_op jit(solution)/shard_map/add | solution.py:18
  138.6 8.4 %fusion.57 = (f32[1,8,32768]{2,1,0:T(8,128)S(1)}, f32[1,8,32768]{2,1,0:T(8,128)S(1)}, f32[1,8,32768]{2,1,0:T(8,128)S(1)}, f32[1,8,32768]{2,1,0:T(8,128)}, f32[1,8,32768]{2,1,0:T(8,128)}, /*index=5*/f32[1,8,32768]{2,1,0:T(8,128)}) fusion(f32[3,8,32768]{2,1,0:T(8,128)S(1)} %get-tuple-element.340, f32[1,8,32768]{2,1,0:T(8,128)S(1)} %copy-done.11, ...), kind=kLoop, calls=%fused_computation.219 | loop fusion | flops 43253760 | bytes 14680076 | tf_op jit(solution)/shard_map/add | solution.py:18
  147.0 7.5 %broadcast_select_fusion.2 = (f32[1,8,32768]{2,1,0:T(8,128)}, pred[1,8,32768]{2,1,0:T(8,128)(4,1)S(1)}, f32[1,8,32768]{2,1,0:T(8,128)}, f32[1,8,32768]{2,1,0:T(8,128)}, f32[1,8,32768]{2,1,0:T(8,128)}) fusion(f32[1,8,32768]{2,1,0:T(8,128)S(1)} %get-tuple-element.101, f32[1,8,32768]{2,1,0:T(8,128)S(1)} %get-tuple-element.100, ...), kind=kLoop, calls=%fused_computation.704 | loop fusion | flops 49807360 | bytes 10747904 | tf_op jit(solution)/shard_map/jit(_where)/select_n | solution.py:26
  154.5 2.5 stack.577
  156.9 4.6 fusion.100
  161.6 2.4 stack.578
  164.0 2.4 stack.579
  166.4 2.2 maximum_reduce_fusion.2
  172.1 4.4 broadcast_select_fusion
  176.6 10.6 %broadcast_select_fusion.4 = (f32[1,8,32768]{2,1,0:T(8,128)}, pred[1,8,32768]{2,1,0:T(8,128)(4,1)}, f32[1,8,32768]{2,1,0:T(8,128)}, f32[1,8,32768]{2,1,0:T(8,128...) fusion(f32[3,8,32768]{2,1,0:T(8,128)S(1)} %get-tuple-element.34, ...), kind=kLoop, calls=%fused_computation.706 | loop fusion | flops 63438848 | bytes 24379392 | tf_op jit(solution)/shard_map/jit(_where)/select_n | solution.py:26
  187.2 2.4 stack.559
  189.6 4.4 fusion.92
  195.2 2.6 stack.561
  197.8 2.1 maximum_reduce_fusion
  203.4 3.0 fusion.104
  210.3 19.7 %collective-permute-done.2 = f32[2,8,16384]{2,1,0:T(8,128)S(1)} collective-permute-done((f32[2,8,16384]{2,1,0:T(8,128)S(1)}, f32[2,8,16384]{2,1,0:T(8,128)S(1)}, u32[]{:S(2)}, u32[]{:S(2)}) %collective-permute-start.2) | collective-permute-done | bytes 1048608 | tf_op jit(solution)/shard_map/ppermute | solution.py:8
  230.3 22.1 %collective-permute-done.3 = f32[2,8,16384]{2,1,0:T(8,128)S(1)} collective-permute-done((f32[2,8,16384]{2,1,0:T(8,128)S(1)}, f32[2,8,16384]{2,1,0:T(8,128)S(1)}, u32[]{:S(2)}, u32[]{:S(2)}) %collective-permute-start.3) | collective-permute-done | bytes 1048608 | tf_op jit(solution)/shard_map/ppermute | solution.py:8
  252.8 3.6 broadcast_select_fusion.8
  256.4 2.0 stack.605
  258.4 3.1 fusion.202
  261.5 1.9 stack.606
  263.4 1.9 stack.607
  270.2 6.8 %fusion.177 = (f32[1,8,16384]{2,1,0:T(8,128)S(1)}, f32[1,8,16384]{2,1,0:T(8,128)S(1)}, f32[1,8,16384]{2,1,0:T(8,128)S(1)}, f32[1,8,16384]{2,1,0:T(8,128)}, f32[1,8,16384]{2,1,0:T(8,128)}, /*index=5*/f32[1,8,16384]{2,1,0:T(8,128)}) fusion(f32[3,8,16384]{2,1,0:T(8,128)S(1)} %get-tuple-element.345, f32[1,8,16384]{2,1,0:T(8,128)} %get-tuple-element.408, ...), kind=kLoop, calls=%fused_computation.618 | loop fusion | flops 21626880 | bytes 7340044 | tf_op jit(solution)/shard_map/add | solution.py:18
  277.0 5.5 %fusion.165 = (f32[1,8,16384]{2,1,0:T(8,128)S(1)}, f32[1,8,16384]{2,1,0:T(8,128)S(1)}, f32[1,8,16384]{2,1,0:T(8,128)S(1)}, f32[1,8,16384]{2,1,0:T(8,128)}, f32[1,8,16384]{2,1,0:T(8,128)}, /*index=5*/f32[1,8,16384]{2,1,0:T(8,128)}) fusion(f32[3,8,16384]{2,1,0:T(8,128)S(1)} %get-tuple-element.347, f32[1,8,16384]{2,1,0:T(8,128)S(1)} %copy-done.26, ...), kind=kLoop, calls=%fused_computation.577 | loop fusion | flops 21626880 | bytes 7340044 | tf_op jit(solution)/shard_map/add | solution.py:18
  282.5 4.2 broadcast_select_fusion.7
  286.6 1.9 stack.614
  288.6 3.1 fusion.208
  291.7 1.9 stack.615
  293.6 1.9 stack.616
  297.2 3.8 broadcast_select_fusion.5
  301.0 5.7 %broadcast_select_fusion.9 = (f32[1,8,16384]{2,1,0:T(8,128)}, pred[1,8,16384]{2,1,0:T(8,128)(4,1)S(1)}, f32[1,8,16384]{2,1,0:T(8,128)}, f32[1,8,16384]{2,1,0:T(8...) fusion(f32[3,8,16384]{2,1,0:T(8,128)S(1)} %get-tuple-element.34, ...), kind=kLoop, calls=%fused_computation.1069 | loop fusion | flops 31719424 | bytes 12189696 | tf_op jit(solution)/shard_map/jit(_where)/select_n | solution.py:26
  307.9 2.3 fusion.212
  311.2 2.7 collective-permute-start.4
  326.0 9.8 %collective-permute-done.5 = f32[2,8,8192]{2,1,0:T(8,128)S(1)} collective-permute-done((f32[2,8,8192]{2,1,0:T(8,128)S(1)}, f32[2,8,8192]{2,1,0:T(8,128)S(1)}, u32[]{:S(2)}, u32[]{:S(2)}) %collective-permute-start.5) | collective-permute-done | bytes 524320 | tf_op jit(solution)/shard_map/ppermute | solution.py:8
  336.0 1.9 broadcast_select_fusion.13
  337.9 1.7 stack.642
  339.6 2.3 fusion.310
  341.9 1.7 stack.643
  343.7 1.7 stack.644
  347.5 5.0 %fusion.285 = (f32[1,8,8192]{2,1,0:T(8,128)S(1)}, f32[1,8,8192]{2,1,0:T(8,128)S(1)}, f32[1,8,8192]{2,1,0:T(8,128)S(1)}, f32[1,8,8192]{2,1,0:T(8,128)}, f32[1,8,8192]{2,1,0:T(8,128)}, /*index=5*/f32[1,8,8192]{2,1,0:T(8,128)}) fusion(f32[3,8,8192]{2,1,0:T(8,128)S(1)} %get-tuple-element.381, f32[1,8,8192]{2,1,0:T(8,128)} %get-tuple-element.456, ...), kind=kLoop, calls=%fused_computation.981 | loop fusion | flops 10813440 | bytes 3670028 | tf_op jit(solution)/shard_map/add | solution.py:18
  352.5 4.0 fusion.273
  356.5 2.3 broadcast_select_fusion.12
  361.3 2.7 broadcast_select_fusion.10
  364.1 3.0 broadcast_select_fusion.14
  384.5 2.9 collective-permute-done.7
  391.8 2.5 fusion.358
  394.4 2.5 fusion.338
  409.8 70.5 %all-reduce = (f32[3,3]{0,1:T(4,128)S(1)}, f32[3,3]{0,1:T(4,128)S(1)}, f32[3,3]{0,1:T(4,128)S(1)}, f32[3,3]{0,1:T(4,128)S(1)}) all-reduce(f32[3,3]{0,1:T(4,128)S(1)} %maximum_maximum_fusion.3, f32[3,3]{0,1:T(4,128)S(1)} %maximum_maximum_fusion.2, f32[3,3]{0,1:T(4,128)S(1)} %maximum_maximum_fusion.1, ...), channel_id=1, replica_groups=mesh['gx'=8,'gy'=16] {'gx','gy'}, use_global_device_ids=true, to_apply=%region_27.28 | all-reduce | flops 36 | bytes 288 | tf_op jit(solution)/shard_map/psum | solution.py:131
  (299 shorter events, 56.7 us)
Async XLA Ops:
  7.1 49.1 %collective-permute-start = (f32[2,8,32768]{2,1,0:T(8,128)}, f32[2,8,32768]{2,1,0:T(8,128)}, u32[]{:S(2)}, u32[]{:S(2)}) collective-permute-start(f32[2,8,32768]{2,1,0:T(8,128)} %pad_maximum_fusion.4), channel_id=1, source_target_pairs={{0,64},{16,80},{32,96},{48,112},{64,0},{80,16},{96,32},{112,48},{1... | collective-permute-start | bytes 6291464 | tf_op jit(solution)/shard_map/ppermute | solution.py:8
  11.4 2.9 copy-start.47
  14.3 86.8 %collective-permute-start.1 = (f32[2,8,32768]{2,1,0:T(8,128)}, f32[2,8,32768]{2,1,0:T(8,128)}, u32[]{:S(2)}, u32[]{:S(2)}) collective-permute-start(f32[2,8,32768]{2,1,0:T(8,128)} %pad_maximum_fusion.5), channel_id=1, source_target_pairs={{0,64},{16,80},{32,96},{48,112},{64,0},{80,16},{96,32},{112,48},{1... | collective-permute-start | bytes 6291464 | tf_op jit(solution)/shard_map/ppermute | solution.py:8
  61.6 43.2 %copy-start.2 = (f32[3,8,32768]{2,1,0:T(8,128)}, f32[3,8,32768]{2,1,0:T(8,128)S(1)}, u32[]{:S(2)}) copy-start(f32[3,8,32768]{2,1,0:T(8,128)S(1)} %get-tuple-element.334) | copy-start | bytes 9437188
  104.8 6.1 %copy-start.3 = (f32[3,8,32768]{2,1,0:T(8,128)}, f32[3,8,32768]{2,1,0:T(8,128)S(1)}, u32[]{:S(2)}) copy-start(f32[3,8,32768]{2,1,0:T(8,128)S(1)} %get-tuple-element.339) | copy-start | bytes 9437188
  122.8 5.6 %copy-start = (f32[3,8,32768]{2,1,0:T(8,128)S(1)}, f32[3,8,32768]{2,1,0:T(8,128)}, u32[]{:S(2)}) copy-start(f32[3,8,32768]{2,1,0:T(8,128)} %get-tuple-element.335) | copy-start | bytes 9437188
  128.4 10.1 %copy-start.4 = (f32[3,8,32768]{2,1,0:T(8,128)S(1)}, f32[3,8,32768]{2,1,0:T(8,128)}, u32[]{:S(2)}) copy-start(f32[3,8,32768]{2,1,0:T(8,128)} %copy-done.3) | copy-start | bytes 9437188
  128.4 10.1 %copy-start.11 = (f32[1,8,32768]{2,1,0:T(8,128)S(1)}, f32[1,8,32768]{2,1,0:T(8,128)}, u32[]{:S(2)}) copy-start(f32[1,8,32768]{2,1,0:T(8,128)} %get-tuple-element.368) | copy-start | bytes 3145732
  128.4 10.1 %copy-start.12 = (f32[1,8,32768]{2,1,0:T(8,128)S(1)}, f32[1,8,32768]{2,1,0:T(8,128)}, u32[]{:S(2)}) copy-start(f32[1,8,32768]{2,1,0:T(8,128)} %get-tuple-element.369) | copy-start | bytes 3145732
  166.4 5.7 %copy-start.22 = (f32[1,8,32768]{2,1,0:T(8,128)S(1)}, f32[1,8,32768]{2,1,0:T(8,128)}, u32[]{:S(2)}) copy-start(f32[1,8,32768]{2,1,0:T(8,128)} %get-tuple-element.331) | copy-start | bytes 3145732
  166.4 5.7 %copy-start.23 = (f32[1,8,32768]{2,1,0:T(8,128)S(1)}, f32[1,8,32768]{2,1,0:T(8,128)}, u32[]{:S(2)}) copy-start(f32[1,8,32768]{2,1,0:T(8,128)} %get-tuple-element.332) | copy-start | bytes 3145732
  166.4 5.7 %copy-start.24 = (f32[1,8,32768]{2,1,0:T(8,128)S(1)}, f32[1,8,32768]{2,1,0:T(8,128)}, u32[]{:S(2)}) copy-start(f32[1,8,32768]{2,1,0:T(8,128)} %get-tuple-element.333) | copy-start | bytes 3145732
  172.1 4.5 copy-start.1
  172.1 4.5 copy-start.13
  172.1 4.5 copy-start.14
  172.1 4.5 copy-start.15
  195.2 8.1 %copy-start.19 = (f32[1,8,32768]{2,1,0:T(8,128)S(1)}, f32[1,8,32768]{2,1,0:T(8,128)}, u32[]{:S(2)}) copy-start(f32[1,8,32768]{2,1,0:T(8,128)} %get-tuple-element.360) | copy-start | bytes 3145732
  195.2 8.2 %copy-start.20 = (f32[1,8,32768]{2,1,0:T(8,128)S(1)}, f32[1,8,32768]{2,1,0:T(8,128)}, u32[]{:S(2)}) copy-start(f32[1,8,32768]{2,1,0:T(8,128)} %get-tuple-element.361) | copy-start | bytes 3145732
  195.2 8.2 %copy-start.21 = (f32[1,8,32768]{2,1,0:T(8,128)S(1)}, f32[1,8,32768]{2,1,0:T(8,128)}, u32[]{:S(2)}) copy-start(f32[1,8,32768]{2,1,0:T(8,128)} %get-tuple-element.363) | copy-start | bytes 3145732
  197.8 5.6 %copy-start.38 = (pred[1,8,32768]{2,1,0:T(8,128)(4,1)S(1)}, pred[1,8,32768]{2,1,0:T(8,128)(4,1)}, u32[]{:S(2)}) copy-start(pred[1,8,32768]{2,1,0:T(8,128)(4,1)} %get-tuple-element.362) | copy-start | bytes 786436
  203.4 3.0 copy-start.18
  206.6 1.6 copy-start.16
  206.6 1.6 copy-start.17
  206.6 1.8 copy-start.25
  206.8 23.2 %collective-permute-start.2 = (f32[2,8,16384]{2,1,0:T(8,128)S(1)}, f32[2,8,16384]{2,1,0:T(8,128)S(1)}, u32[]{:S(2)}, u32[]{:S(2)}) collective-permute-start(f32[2,8,16384]{2,1,0:T(8,128)S(1)} %pad_maximum_fusion.10), channel_id=1, source_target_pairs={{0,32},{16,48},{32,0},{48,16},{64,96},{80,112},{96,64},{112,80},{1... | collective-permute-start | bytes 3145736 | tf_op jit(solution)/shard_map/ppermute | solution.py:8
  208.8 43.7 %collective-permute-start.3 = (f32[2,8,16384]{2,1,0:T(8,128)S(1)}, f32[2,8,16384]{2,1,0:T(8,128)S(1)}, u32[]{:S(2)}, u32[]{:S(2)}) collective-permute-start(f32[2,8,16384]{2,1,0:T(8,128)S(1)} %pad_maximum_fusion.11), channel_id=1, source_target_pairs={{0,32},{16,48},{32,0},{48,16},{64,96},{80,112},{96,64},{112,80},{1... | collective-permute-start | bytes 3145736 | tf_op jit(solution)/shard_map/ppermute | solution.py:8
  230.3 22.5 %copy-start.5 = (f32[3,8,16384]{2,1,0:T(8,128)}, f32[3,8,16384]{2,1,0:T(8,128)S(1)}, u32[]{:S(2)}) copy-start(f32[3,8,16384]{2,1,0:T(8,128)S(1)} %get-tuple-element.344) | copy-start | bytes 4718596
  252.8 3.6 copy-start.6
  270.2 6.8 %copy-start.7 = (f32[3,8,16384]{2,1,0:T(8,128)S(1)}, f32[3,8,16384]{2,1,0:T(8,128)}, u32[]{:S(2)}) copy-start(f32[3,8,16384]{2,1,0:T(8,128)} %copy-done.6) | copy-start | bytes 4718596
  270.2 6.8 %copy-start.26 = (f32[1,8,16384]{2,1,0:T(8,128)S(1)}, f32[1,8,16384]{2,1,0:T(8,128)}, u32[]{:S(2)}) copy-start(f32[1,8,16384]{2,1,0:T(8,128)} %get-tuple-element.410) | copy-start | bytes 1572868
  270.2 6.8 %copy-start.27 = (f32[1,8,16384]{2,1,0:T(8,128)S(1)}, f32[1,8,16384]{2,1,0:T(8,128)}, u32[]{:S(2)}) copy-start(f32[1,8,16384]{2,1,0:T(8,128)} %get-tuple-element.411) | copy-start | bytes 1572868
  297.1 3.9 copy-start.34
  297.1 3.9 copy-start.35
  297.1 3.9 copy-start.36
  306.7 3.5 copy-start.33
  310.1 3.8 copy-start.31
  310.1 3.8 copy-start.32
  310.2 3.8 copy-start.37
  310.3 3.7 copy-start.10
  310.3 5.0 %copy-start.28 = (f32[1,8,16384]{2,1,0:T(8,128)S(1)}, f32[1,8,16384]{2,1,0:T(8,128)}, u32[]{:S(2)}) copy-start(f32[1,8,16384]{2,1,0:T(8,128)} %get-tuple-element.117) | copy-start | bytes 1572868
  310.3 5.0 %copy-start.29 = (f32[1,8,16384]{2,1,0:T(8,128)S(1)}, f32[1,8,16384]{2,1,0:T(8,128)}, u32[]{:S(2)}) copy-start(f32[1,8,16384]{2,1,0:T(8,128)} %get-tuple-element.118) | copy-start | bytes 1572868
  310.3 5.0 %copy-start.30 = (f32[1,8,16384]{2,1,0:T(8,128)S(1)}, f32[1,8,16384]{2,1,0:T(8,128)}, u32[]{:S(2)}) copy-start(f32[1,8,16384]{2,1,0:T(8,128)} %get-tuple-element.119) | copy-start | bytes 1572868
  311.2 13.5 %collective-permute-start.4 = (f32[2,8,8192]{2,1,0:T(8,128)}, f32[2,8,8192]{2,1,0:T(8,128)S(1)}, u32[]{:S(2)}, u32[]{:S(2)}) collective-permute-start(f32[2,8,8192]{2,1,0:T(8,128)} %pad_maximum_fusion.16), channel_id=1, source_target_pairs={{0,8},{1,9},{2,10},{3,11},{4,12},{5,13},{6,14},{7,15},{8,0},{9,1},... | collective-permute-start | bytes 1572872 | tf_op jit(solution)/shard_map/ppermute | solution.py:8
  314.1 1.1 copy-start.8
  316.5 19.4 %copy-start.9 = (f32[3,8,16384]{2,1,0:T(8,128)S(1)}, f32[3,8,16384]{2,1,0:T(8,128)}, u32[]{:S(2)}) copy-start(f32[3,8,16384]{2,1,0:T(8,128)} %copy-done.8) | copy-start | bytes 4718596
  323.4 12.5 %collective-permute-start.5 = (f32[2,8,8192]{2,1,0:T(8,128)S(1)}, f32[2,8,8192]{2,1,0:T(8,128)S(1)}, u32[]{:S(2)}, u32[]{:S(2)}) collective-permute-start(f32[2,8,8192]{2,1,0:T(8,128)S(1)} %pad_maximum_fusion.17), channel_id=1, source_target_pairs={{0,8},{1,9},{2,10},{3,11},{4,12},{5,13},{6,14},{7,15},{8,0},{9,1},... | collective-permute-start | bytes 1572872 | tf_op jit(solution)/shard_map/ppermute | solution.py:8
  345.4 7.2 %copy-start.39 = (f32[1,8,8192]{2,1,0:T(8,128)S(1)}, f32[1,8,8192]{2,1,0:T(8,128)}, u32[]{:S(2)}) copy-start(f32[1,8,8192]{2,1,0:T(8,128)} %get-tuple-element.459) | copy-start | bytes 786436
  358.9 5.2 %copy-start.40 = (f32[1,8,8192]{2,1,0:T(8,128)S(1)}, f32[1,8,8192]{2,1,0:T(8,128)}, u32[]{:S(2)}) copy-start(f32[1,8,8192]{2,1,0:T(8,128)} %get-tuple-element.412) | copy-start | bytes 786436
  358.9 5.2 %copy-start.41 = (f32[1,8,8192]{2,1,0:T(8,128)S(1)}, f32[1,8,8192]{2,1,0:T(8,128)}, u32[]{:S(2)}) copy-start(f32[1,8,8192]{2,1,0:T(8,128)} %get-tuple-element.413) | copy-start | bytes 786436
  358.9 5.2 %copy-start.42 = (f32[1,8,8192]{2,1,0:T(8,128)S(1)}, f32[1,8,8192]{2,1,0:T(8,128)}, u32[]{:S(2)}) copy-start(f32[1,8,8192]{2,1,0:T(8,128)} %get-tuple-element.414) | copy-start | bytes 786436
  367.1 3.9 copy-start.45
  367.2 3.9 copy-start.46
  367.2 4.9 %copy-start.43 = (f32[1,8,8192]{2,1,0:T(8,128)S(1)}, f32[1,8,8192]{2,1,0:T(8,128)}, u32[]{:S(2)}) copy-start(f32[1,8,8192]{2,1,0:T(8,128)} %get-tuple-element.173) | copy-start | bytes 786436
  367.2 4.9 %copy-start.44 = (f32[1,8,8192]{2,1,0:T(8,128)S(1)}, f32[1,8,8192]{2,1,0:T(8,128)}, u32[]{:S(2)}) copy-start(f32[1,8,8192]{2,1,0:T(8,128)} %get-tuple-element.174) | copy-start | bytes 786436
  369.8 3.2 copy-start.48
  370.5 13.0 %collective-permute-start.6 = (f32[2,8,4096]{2,1,0:T(8,128)}, f32[2,8,4096]{2,1,0:T(8,128)}, u32[]{:S(2)}, u32[]{:S(2)}) collective-permute-start(f32[2,8,4096]{2,1,0:T(8,128)} %pad_maximum_fusion.22), channel_id=1, source_target_pairs={{0,4},{1,5},{2,6},{3,7},{4,0},{5,1},{6,2},{7,3},{8,12},{9,13},{10,... | collective-permute-start | bytes 786440 | tf_op jit(solution)/shard_map/ppermute | solution.py:8
  382.1 5.3 %collective-permute-start.7 = (f32[2,8,4096]{2,1,0:T(8,128)S(1)}, f32[2,8,4096]{2,1,0:T(8,128)S(1)}, u32[]{:S(2)}, u32[]{:S(2)}) collective-permute-start(f32[2,8,4096]{2,1,0:T(8,128)S(1)} %pad_maximum_fusion.23), channel_id=1, source_target_pairs={{0,4},{1,5},{2,6},{3,7},{4,0},{5,1},{6,2},{7,3},{8,12},{9,13},{10,... | collective-permute-start | bytes 786440 | tf_op jit(solution)/shard_map/ppermute | solution.py:8
where the time goes:
time: 492 us; the launch traced here: 483 us
  other arithmetic  174 us (35%)
  waiting for transfers between devices  121 us (25%)
  blocking collectives  70.5 us (14%)
  local copies, waits for them, and re-layouts  63.8 us (13%)
  between operations  40.8 us (8%)
  starting transfers between devices  12.3 us (2%)
    ppermute x8, waiting for transfers between devices, from_partner(): lax.ppermute(x, axis, [(i, i ^ 1 << stride) for i in range(lax.axis_size(...  121 us
    psum x1, blocking collectives, publish(): summed = lax.psum(points, ('gx', 'gy'))  70.5 us
    select_n x31, other arithmetic, settle(): jnp.where(at_modulus, nothing, lowest)  58.3 us
    another operation x40, local copies, waits for them, and re-layouts, settle(): jnp.stack([jnp.where(at_modulus, nothing, lowest), jnp.where(at_modulus,...  39.9 us
    add x6, other arithmetic, settle(): highest = highest + carried  39.7 us
    select_n x33, other arithmetic, settle(): jnp.where(at_modulus, nothing, middle)  34.2 us
    reduce_sum x24, other arithmetic, field_sum(): summed = values.reshape(3, length // stride, stride).sum(axis=2)  13.1 us
    ppermute x8, starting transfers between devices, from_partner(): lax.ppermute(x, axis, [(i, i ^ 1 << stride) for i in range(lax.axis_size(...  12.3 us
  transfers between devices with their start and end apart: 8, of which 6 were waited for; matrix products, arithmetic and copies ran while one was open for 5% of the time, Pallas kernels for 0%

commit v1 on v0

v1 whole, which is shorter than its diff:
```python
import jax
import jax.numpy as jnp
from jax import lax
from jax.experimental import pallas as pl
from jax.experimental.pallas import tpu as pltpu
from jax.sharding import PartitionSpec as P

MESH = pl.DeviceIdType.MESH
I32 = jnp.int32
F32 = jnp.float32
MODULUS = 0x7FFFFFFF
STEPS = 8
TILES = 16
PART = 4


def srl(x, n):
    return lax.shift_right_logical(x, jnp.full(x.shape, n, I32))


def fold31(x):
    return (x & MODULUS) + srl(x, 31)


def encode(v):
    scaled = lax.shift_left((v & 0x7FFFFF) | 0x800000, srl(v, 23) & 7)
    power = lax.shift_left(jnp.full(v.shape, 1, I32), srl(v, 26) & 15).astype(F32)
    power = power * power
    power = power * power
    power = power * power
    unit = jnp.where(v >= 1 << 30, F32(-(2.0**-60)), F32(2.0**-60))
    return scaled.astype(F32) * unit * power


def decode(x):
    negative = x < 0
    a = jnp.abs(x)
    high = a >= F32(2.0**27)
    v = jnp.where(high, I32((1 << 29) - (1 << 23)), I32(-(1 << 23)))
    a = a * jnp.where(high, F32(2.0**-4), F32(2.0**60))
    for bit, shift in ((28, 32), (27, 16), (26, 8)):
        high = a >= F32(2.0 ** (23 + shift))
        v = v + jnp.where(high, I32(1 << bit), I32(0))
        a = a * jnp.where(high, F32(2.0**-shift), F32(1.0))
    v = v + jnp.where(negative, I32(1 << 30), I32(0))
    scaled = a.astype(I32)
    low = 8 - lax.clz(scaled)
    return v + lax.shift_right_logical(scaled, low) + lax.shift_left(low, jnp.full(low.shape, 23, I32))


def split(v):
    return v & 0xFFFF, srl(v, 16)


def difference(a, b):
    d = a - b
    return jnp.where(d < 0, d + MODULUS, d)


def add_product(sums, a, b):
    low = a[0] * b[0]
    middle = a[0] * b[1] + a[1] * b[0]
    high = (a[1] + a[1]) * b[1]
    return (
        sums[0] + ((low & 0xFFFF) + srl(middle, 15) + (high & 0xFFFF)),
        sums[1] + (srl(low, 16) + (middle & 0x7FFF) + srl(high, 16)),
    )


def folded(base, d, scalar):
    low = d[0] * scalar[0]
    middle = d[0] * scalar[1] + d[1] * scalar[0]
    t = fold31(low) + srl(middle, 15)
    t = fold31(t + d[1] * scalar[2])
    t = fold31(t + lax.shift_left(middle & 0x7FFF, jnp.full(middle.shape, 16, I32)))
    return fold31(t + base)


def two_rounds(selects, proofs, sums, scalars):
    select_parts, proof_parts = [split(v) for v in selects], [split(v) for v in proofs]
    sums = list(sums)
    for i in range(4):
        sums[i] = add_product(sums[i], select_parts[i], proof_parts[i])
    select_next, proof_next = [], []
    for pair in range(2):
        ds = split(difference(selects[2 * pair + 1], selects[2 * pair]))
        dp = split(difference(proofs[2 * pair + 1], proofs[2 * pair]))
        sums[4] = add_product(sums[4], ds, dp)
        select_next.append(folded(selects[2 * pair], ds, scalars[pair]))
        proof_next.append(folded(proofs[2 * pair], dp, scalars[pair]))
    for i in range(2):
        sums[5 + i] = add_product(sums[5 + i], split(select_next[i]), split(proof_next[i]))
    ds = split(difference(select_next[1], select_next[0]))
    dp = split(difference(proof_next[1], proof_next[0]))
    sums[7] = add_product(sums[7], ds, dp)
    return folded(select_next[0], ds, scalars[2]), folded(proof_next[0], dp, scalars[2]), tuple(sums)


def scalar_parts(challenge, flipped):
    other = 1 - challenge
    other = other + (lax.shift_right_arithmetic(other, I32(31)) & MODULUS)
    value = challenge * (1 - flipped) + other * flipped
    low, high = value & 0xFFFF, lax.shift_right_logical(value, I32(16))
    return [jnp.full((8, 128), s, I32) for s in (low, high, high + high)]


def across_tile(x):
    for shift in (64, 32, 16, 8, 4, 2, 1):
        x = x + pltpu.roll(x, shift, 1)
    return x


def kernel(
    challenges, selectors, proofs, out_points, out_selects, out_proofs,
    raw, y_send, y_recv, x_own, x_send, x_recv, sums_ref, done, gathered, gathered_z, tile_out,
    raw_sem, y_send_sem, y_recv_sem, x_send_sem, x_recv_sem, plane_send_sem, plane_recv_sem, z_send_sem, z_recv_sem, out_sem,
):
    gx, gy = lax.axis_index("gx"), lax.axis_index("gy")
    y, z_low = gx // 2, gx % 2
    x, z_core = gy // 4, gy % 4

    def plane_peer(dy, dx):
        return {"gx": (y + dy) % 4 * 2 + z_low, "gy": (x + dx) % 4 * 4 + z_core}

    def z_peer(m):
        z_high, core = z_core // 2, z_core % 2
        return {
            "gx": y * 2 + (z_low + m % 2) % 2,
            "gy": x * 4 + (z_high + m // 2 % 2) % 2 * 2 + (core + m // 4) % 2,
        }

    def load(step, table):
        source = (selectors, proofs)[table]
        return pltpu.make_async_copy(source.at[:, step], raw.at[step, table], raw_sem.at[step, table])

    def y_copy(step, k):
        return pltpu.make_async_remote_copy(
            y_send.at[step, k], y_recv.at[step, k], y_send_sem.at[step, k], y_recv_sem.at[step, k],
            device_id=plane_peer(k + 1, 0), device_id_type=MESH,
        )

    def x_copy(step, k):
        return pltpu.make_async_remote_copy(
            x_send.at[step, k], x_recv.at[step, k], x_send_sem.at[step, k], x_recv_sem.at[step, k],
            device_id=plane_peer(0, k + 1), device_id_type=MESH,
        )

    barrier = pltpu.get_barrier_semaphore()
    for m in range(1, 16):
        pl.semaphore_signal(barrier, 1, device_id=plane_peer(m // 4, m % 4), device_id_type=MESH)
    for m in range(1, 8):
        pl.semaphore_signal(barrier, 1, device_id=z_peer(m), device_id_type=MESH)

    for step in range(STEPS):
        for table in range(2):
            load(step, table).start()

    def raw_value(step, table, tile):
        low, middle, high = (raw[step, table, limb, tile].astype(I32) for limb in range(3))
        return low + lax.shift_left(middle, jnp.full(low.shape, 11, I32)) + lax.shift_left(high, jnp.full(low.shape, 22, I32))

    def prepare(step):
        for table in range(2):
            load(step, table).wait()

        def body(i, carry):
            k, t = i // TILES, i % TILES
            tile = (y + k + 1) % 4 * TILES + t
            for table in range(2):
                y_send[step, k, table, t] = encode(raw_value(step, table, tile))
            return carry

        lax.fori_loop(0, 3 * TILES, body, 0)

    def send(step):
        for k in range(3):
            y_copy(step, k).start()

    prepare(0)
    pl.semaphore_wait(barrier, 22)
    send(0)

    def ahead(step, carry):
        prepare(step)
        send(step)
        return carry

    lax.fori_loop(1, STEPS, ahead, 0)

    sums_ref[...] = jnp.zeros_like(sums_ref)

    def phase_scalars(position, first, second):
        behind = (position + 3) % 4
        return [
            scalar_parts(challenges[first], position // 2),
            scalar_parts(challenges[first], behind // 2),
            scalar_parts(challenges[second], position % 2),
        ]

    def load_sums(phase):
        return tuple((sums_ref[phase, i, 0], sums_ref[phase, i, 1]) for i in range(8))

    def store_sums(phase, sums):
        for i in range(8):
            for part in range(2):
                sums_ref[phase, i, part] = sums[i][part]

    y_scalars = phase_scalars(y, 0, 1)
    x_scalars = phase_scalars(x, 2, 3)

    def y_phase(step):
        for k in range(3):
            y_copy(step, k).wait_recv()

        def body(i, sums):
            part, t = i // PART, i % PART
            tile = (x + part) % 4 * PART + t
            tables = [
                [raw_value(step, table, y * TILES + tile)]
                + [decode(y_recv[step, k, table, tile]) for k in (1, 0, 2)]
                for table in range(2)
            ]
            select, proof, sums = two_rounds(tables[0], tables[1], sums, y_scalars)
            x_own[0, i], x_own[1, i] = select, proof
            return sums

        store_sums(0, lax.fori_loop(0, TILES, body, load_sums(0)))

        def coded(i, carry):
            k, t = i // PART, i % PART
            for table in range(2):
                x_send[step, k, table, t] = encode(x_own[table, PART + i])
            return carry

        lax.fori_loop(0, 3 * PART, coded, 0)
        for k in range(3):
            x_copy(step, k).start()
        for t in range(PART):
            for table in range(2):
                x_own[table, TILES + step * PART + t] = x_own[table, t]

    def x_phase(step):
        for k in range(3):
            x_copy(step, k).wait_recv()

        def body(t, sums):
            tables = [
                [x_own[table, TILES + step * PART + t]] + [decode(x_recv[step, k, table, t]) for k in (1, 0, 2)]
                for table in range(2)
            ]
            select, proof, sums = two_rounds(tables[0], tables[1], sums, x_scalars)
            for table, value in ((0, select), (1, proof)):
                done[table, step, t] = jnp.where(value == MODULUS, 0, value)
            return sums

        store_sums(1, lax.fori_loop(0, PART, body, load_sums(1)))

    def main(step, carry):
        y_phase(step)

        @pl.when(step >= 1)
        def _():
            x_phase(step - 1)

        return carry

    lax.fori_loop(0, STEPS, main, 0)
    x_phase(STEPS - 1)

    outs = [
        pltpu.make_async_copy(done.at[table], (out_selects, out_proofs)[table], out_sem.at[table]) for table in range(2)
    ]
    for copy in outs:
        copy.start()

    row = lax.broadcasted_iota(I32, (8, 128), 0)
    lane = lax.broadcasted_iota(I32, (8, 128), 1)
    halves = [[jnp.zeros((8, 128), I32) for _ in range(2)] for _ in range(3)]
    for phase, position in ((0, y), (1, x)):
        own_high, behind_high, odd = position // 2, (position + 3) % 4 // 2, position % 2
        sums = load_sums(phase)
        points = []
        for part in range(2):
            own, ahead_two, behind, ahead_one, across, even_sum, odd_sum, across_next = (s[part] for s in sums)
            upper = own * own_high + ahead_two * (1 - own_high) + behind * behind_high + ahead_one * (1 - behind_high)
            lower = own + ahead_two + behind + ahead_one - upper
            second_upper = even_sum * odd + odd_sum * (1 - odd)
            second_lower = even_sum + odd_sum - second_upper
            points.append((lower, upper, across, second_lower, second_upper, across_next))
        for i in range(6):
            at_round, at_point = 2 * phase + i // 3, i % 3
            low, high = points[0][i], points[1][i]
            value = fold31(low + srl(high, 15) + lax.shift_left(high & 0x7FFF, jnp.full(high.shape, 16, I32)))
            for half, piece in enumerate(split(value)):
                for shift in (4, 2, 1):
                    piece = piece + pltpu.roll(piece, shift, 0)
                halves[at_point][half] += jnp.where(row == at_round, piece, 0)
    tile = jnp.zeros((8, 128), I32)
    for at_point in range(3):
        low, high = (across_tile(half) for half in halves[at_point])
        value = fold31(low + srl(high, 15))
        value = fold31(value + lax.shift_left(high & 0x7FFF, jnp.full(high.shape, 16, I32)))
        for limb, piece in enumerate((value & 2047, srl(value, 11) & 2047, srl(value, 22))):
            tile += jnp.where(lane == 3 * limb + at_point, piece, 0)
    tile_out[0] = tile.astype(F32)

    def plane_copy(m):
        return pltpu.make_async_remote_copy(
            tile_out.at[0], gathered.at[m], plane_send_sem.at[m], plane_recv_sem.at[m],
            device_id=plane_peer(m // 4, m % 4), device_id_type=MESH,
        )

    def z_copy(m):
        return pltpu.make_async_remote_copy(
            tile_out.at[1], gathered_z.at[m], z_send_sem.at[m], z_recv_sem.at[m],
            device_id=z_peer(m), device_id_type=MESH,
        )

    for m in range(1, 16):
        plane_copy(m).start()
    total = tile_out[0]
    for m in range(1, 16):
        plane_copy(m).wait_recv()
        total = total + gathered[m]
    tile_out[1] = total
    for m in range(1, 8):
        z_copy(m).start()
    for m in range(1, 8):
        z_copy(m).wait_recv()
        total = total + gathered_z[m]

    limbs = total.astype(I32)
    middle, high = pltpu.roll(limbs, 125, 1), pltpu.roll(limbs, 122, 1)
    value = limbs + lax.shift_left(middle, jnp.full(middle.shape, 11, I32))
    value = fold31(value + srl(high, 9))
    value = fold31(value + lax.shift_left(high & 511, jnp.full(high.shape, 22, I32)))
    at_zero, at_one = pltpu.roll(value, 2, 1), pltpu.roll(value, 1, 1)
    at_two = fold31(fold31(value + value) + fold31(at_one + at_one))
    at_two = fold31(at_two + (MODULUS - at_zero))
    value = jnp.where(lane == 2, at_two, value)
    value = jnp.where(value == MODULUS, 0, value)
    for limb, piece in enumerate((value & 2047, srl(value, 11) & 2047, srl(value, 22))):
        out_points[limb] = piece.astype(F32)[:4, :3]

    for copy in outs:
        copy.wait()

    def finish(step, carry):
        for k in range(3):
            y_copy(step, k).wait_send()
            x_copy(step, k).wait_send()
        return carry

    lax.fori_loop(0, STEPS, finish, 0)
    for m in range(1, 16):
        plane_copy(m).wait_send()
    for m in range(1, 8):
        z_copy(m).wait_send()


def shards(selectors, proofs, challenges):
    points, selects, proofs_done = pl.pallas_call(
        kernel,
        out_shape=(
            jax.ShapeDtypeStruct((3, 4, 3), F32),
            jax.ShapeDtypeStruct((STEPS, PART, 8, 128), I32),
            jax.ShapeDtypeStruct((STEPS, PART, 8, 128), I32),
        ),
        in_specs=[
            pl.BlockSpec(memory_space=pltpu.SMEM),
            pl.BlockSpec(memory_space=pltpu.HBM),
            pl.BlockSpec(memory_space=pltpu.HBM),
        ],
        out_specs=(
            pl.BlockSpec(memory_space=pltpu.VMEM),
            pl.BlockSpec(memory_space=pltpu.HBM),
            pl.BlockSpec(memory_space=pltpu.HBM),
        ),
        scratch_shapes=[
            pltpu.VMEM((STEPS, 2, 3, 64, 8, 128), F32),
            pltpu.VMEM((STEPS, 3, 2, TILES, 8, 128), F32),
            pltpu.VMEM((STEPS, 3, 2, TILES, 8, 128), F32),
            pltpu.VMEM((2, TILES + STEPS * PART, 8, 128), I32),
            pltpu.VMEM((STEPS, 3, 2, PART, 8, 128), F32),
            pltpu.VMEM((STEPS, 3, 2, PART, 8, 128), F32),
            pltpu.VMEM((2, 8, 2, 8, 128), I32),
            pltpu.VMEM((2, STEPS, PART, 8, 128), I32),
            pltpu.VMEM((16, 8, 128), F32),
            pltpu.VMEM((8, 8, 128), F32),
            pltpu.VMEM((2, 8, 128), F32),
            pltpu.SemaphoreType.DMA((STEPS, 2)),
            pltpu.SemaphoreType.DMA((STEPS, 3)),
            pltpu.SemaphoreType.DMA((STEPS, 3)),
            pltpu.SemaphoreType.DMA((STEPS, 3)),
            pltpu.SemaphoreType.DMA((STEPS, 3)),
            pltpu.SemaphoreType.DMA((16,)),
            pltpu.SemaphoreType.DMA((16,)),
            pltpu.SemaphoreType.DMA((8,)),
            pltpu.SemaphoreType.DMA((8,)),
            pltpu.SemaphoreType.DMA((2,)),
        ],
        compiler_params=pltpu.CompilerParams(collective_id=0, has_side_effects=True, vmem_limit_bytes=60 << 20),
        name="sumcheck",
    )(challenges, selectors.reshape(3, 8, 64, 8, 128), proofs.reshape(3, 8, 64, 8, 128))

    def limbs(values):
        values = jnp.broadcast_to(values.reshape(1, 8, 32, 128), (3, 8, 32, 128))
        place = lax.broadcasted_iota(I32, values.shape, 0)
        return (lax.shift_right_logical(values, 11 * place) & 2047).astype(F32).reshape(3, 8, 1, 1, 4096)

    return points, limbs(selects), limbs(proofs_done)


def solution(mesh):
    tables = P(None, None, "gx", "gy", None)
    return jax.shard_map(shards, mesh=mesh, in_specs=(tables, tables, P()), out_specs=(P(), tables, tables), check_vma=False)
```

time: 492 us -> 79.2 us (0.16); the launches traced: 483 us -> 79 us
  other arithmetic: 174 us -> 1.73 us
  waiting for transfers between devices: 121 us -> 0 us
  Pallas kernels: 0 us -> 74.2 us
  blocking collectives: 70.5 us -> 0 us
  local copies, waits for them, and re-layouts: 63.8 us -> 2.41 us
  between operations: 40.8 us -> 0.65 us
  starting transfers between devices: 12.3 us -> 0 us
    ppermute x8 -> x0, waiting for transfers between devices: 121 us -> none  [from_partner(): lax.ppermute(x, axis, [(i, i ^ 1 << stride) for i in range(lax.axis_size(...]
    select_n x72 -> x0, other arithmetic: 100 us -> none  [the longest x31 58.3 us: settle(): jnp.where(at_modulus, nothing, lowest)]
    pallas_call x0 -> x1, Pallas kernels: none -> 74.2 us  [shards(): pl.pallas_call(kernel, out_shape=(jax.ShapeDtypeStruct((3, 4, 3), F32), j...]
    psum x1 -> x0, blocking collectives: 70.5 us -> none  [publish(): summed = lax.psum(points, ('gx', 'gy'))]
    add x52 -> x0, other arithmetic: 48.2 us -> none  [the longest x6 39.7 us: settle(): highest = highest + carried]
    another operation x40 -> x0, local copies, waits for them, and re-layouts: 39.9 us -> none  [settle(): jnp.stack([jnp.where(at_modulus, nothing, lowest), jnp.where(at_modulus,...]
    slice x18 -> x0, local copies, waits for them, and re-layouts: 13.9 us -> none  [the longest x12 7.61 us: field_sum(): values = settle(summed[0], summed[1], summed[2])]
    reduce_sum x24 -> x0, other arithmetic: 13.1 us -> none  [field_sum(): summed = values.reshape(3, length // stride, stride).sum(axis=2)]
  transfers between devices with their start and end apart: 8 -> 0, of which waited for: 6 -> 0; matrix products, arithmetic and copies ran while one was open for 5% -> 0% of each run, Pallas kernels for 0% -> 0%
where the time goes in v1:
time: 79.2 us; the launch traced here: 79 us
  Pallas kernels  74.2 us (94%)
  local copies, waits for them, and re-layouts  2.41 us (3%)
  other arithmetic  1.73 us (2%)
    pallas_call x1, Pallas kernels, shards(): pl.pallas_call(kernel, out_shape=(jax.ShapeDtypeStruct((3, 4, 3), F32), j...  74.2 us
    convert_element_type x1, other arithmetic, limbs(): (lax.shift_right_logical(values, 11 * place) & 2047).astype(F32)  1.72 us

profile of v1, /device:TPU:1, one launch (start us, length us, event | category | flops | bytes accessed | tf_op | source)
XLA Modules:
  0.0 79.0 jit_solution(13071942868809455403)
XLA Ops:
  0.6 74.2 %sumcheck.1 = (f32[3,4,3]{2,1,0:T(4,128)}, s32[8,4,8,128]{3,2,1,0:T(8,128)}, s32[8,4,8,128]{3,2,1,0:T(8,128)}) custom-call(s32[4]{0:T(128)} %challenges.1, f32[3,8,64,8,128]{4,3,2,1,0:T(8,128)} %bitcast.10, f32[3,8,64,8,128]{4,3,2,1,0:T(8,128)} %bitcast.11), custom_call_target="tpu_custom_call" | custom-call | tf_op jit(solution)/shard_map/sumcheck/pallas_call | solution.py:362
  74.9 1.1 %copy_bitcast_fusion = (s32[8,4096]{1,0:T(8,128)S(1)}, s32[8,4096]{1,0:T(8,128)S(1)}) fusion(s32[1,8,32,128]{3,2,1,0:T(8,128)} %bitcast.13, s32[1,8,32,128]{3,2,1,0:T(8,128)} %bitcast.12), kind=kLoop, calls=%fused_computation.2 | loop fusion | bytes 524288 | tf_op jit(solution)/shard_map/broadcast_in_dim | solution.py:407
  76.0 1.7 %and_convert_fusion = (f32[3,8,1,1,4096]{4,3,2,1,0:T(1,128)}, f32[3,8,1,1,4096]{4,3,2,1,0:T(1,128)}) fusion(s32[8,4096]{1,0:T(8,128)S(1)} %get-tuple-element.11, s32[3]{0:T(128)S(1)} %iota_multiply_fusion, s32[8,4096]{1,0:T(8,128)S(1)} %get-tuple-element.12), kind=kLoop, calls=%fused_computation | loop fusion | flops 589824 | bytes 1048588 | tf_op jit(solution)/shard_map/convert_element_type | solution.py:409
  77.7 1.3 %copy.11 = f32[3,4,3]{2,1,0:T(4,128)} copy(f32[3,4,3]{2,1,0:T(4,128)} %get-tuple-element.16) | data formatting | bytes 288
  (1 shorter events, 0.0 us)

commit v2 on v1

--- a/solution.py
+++ b/solution.py
@@ -10,8 +10,10 @@
 F32 = jnp.float32
 MODULUS = 0x7FFFFFFF
 STEPS = 8
+LAST = STEPS - 1
 TILES = 16
 PART = 4
+NEAR = (1, 3, 4)
 
 
 def srl(x, n):
@@ -112,8 +114,9 @@
 
 def kernel(
     challenges, selectors, proofs, out_points, out_selects, out_proofs,
-    raw, y_send, y_recv, x_own, x_send, x_recv, sums_ref, done, gathered, gathered_z, tile_out,
-    raw_sem, y_send_sem, y_recv_sem, x_send_sem, x_recv_sem, plane_send_sem, plane_recv_sem, z_send_sem, z_recv_sem, out_sem,
+    raw, own, y_send, y_recv, early_send, early_recv, x_own, x_send, x_recv, sums_ref, gathered, gathered_z, tile_out,
+    raw_sem, y_send_sem, y_recv_sem, early_send_sem, early_recv_sem, x_send_sem, x_recv_sem,
+    plane_send_sem, plane_recv_sem, z_send_sem, z_recv_sem, token_sem,
 ):
     gx, gy = lax.axis_index("gx"), lax.axis_index("gy")
     y, z_low = gx // 2, gx % 2
@@ -145,11 +148,25 @@
             device_id=plane_peer(0, k + 1), device_id_type=MESH,
         )
 
+    def early_copy(k):
+        return pltpu.make_async_remote_copy(
+            early_send.at[k], early_recv.at[k], early_send_sem.at[k], early_recv_sem.at[k],
+            device_id=plane_peer(0, k + 1), device_id_type=MESH,
+        )
+
     barrier = pltpu.get_barrier_semaphore()
-    for m in range(1, 16):
-        pl.semaphore_signal(barrier, 1, device_id=plane_peer(m // 4, m % 4), device_id_type=MESH)
-    for m in range(1, 8):
-        pl.semaphore_signal(barrier, 1, device_id=z_peer(m), device_id_type=MESH)
+    for m in range(1, 4):
+        pl.semaphore_signal(barrier, 1, device_id=plane_peer(m, 0), device_id_type=MESH)
+        pl.semaphore_signal(barrier, 1, device_id=plane_peer(0, m), device_id_type=MESH)
+        pl.semaphore_signal(barrier, 1, device_id=z_peer(NEAR[m - 1]), device_id_type=MESH)
+
+    def tokens(turn):
+        for m in range(3):
+            pl.semaphore_signal(token_sem.at[turn, m], 1, device_id=z_peer(NEAR[m]), device_id_type=MESH)
+
+    def await_tokens(turn):
+        for m in range(3):
+            pl.semaphore_wait(token_sem.at[turn, m], 1)
 
     for step in range(STEPS):
         for table in range(2):
@@ -172,20 +189,73 @@
 
         lax.fori_loop(0, 3 * TILES, body, 0)
 
+        def mine(t, carry):
+            for table in range(2):
+                own[step, table, t] = encode(raw_value(step, table, y * TILES + t))
+            return carry
+
+        lax.fori_loop(0, TILES, mine, 0)
+
     def send(step):
         for k in range(3):
             y_copy(step, k).start()
-
-    prepare(0)
-    pl.semaphore_wait(barrier, 22)
-    send(0)
 
     def ahead(step, carry):
         prepare(step)
         send(step)
         return carry
 
-    lax.fori_loop(1, STEPS, ahead, 0)
+    def prepare_early():
+        for table in range(2):
+            load(LAST, table).wait()
+
+        def body(i, carry):
+            k, quarter, t = i // TILES, i % TILES // PART, i % PART
+            tile = quarter * TILES + (x + k + 1) % 4 * PART + t
+            for table in range(2):
+                early_send[k, table, quarter, t] = encode(raw_value(LAST, table, tile))
+            return carry
+
+        lax.fori_loop(0, 3 * TILES, body, 0)
+        for k in range(3):
+            early_copy(k).start()
+
+        def mine(i, carry):
+            k, t = i // PART, i % PART
+            for table in range(2):
+                y_send[LAST, k, table, t] = encode(raw_value(LAST, table, (y + k + 1) % 4 * TILES + x * PART + t))
+            return carry
+
+        lax.fori_loop(0, 3 * PART, mine, 0)
+        for t in range(PART):
+            for table in range(2):
+                own[LAST, table, t] = encode(raw_value(LAST, table, y * TILES + x * PART + t))
+
+    def prepare_last():
+        for k in range(3):
+            early_copy(k).wait_recv()
+
+        def body(i, carry):
+            k, t = i // PART, i % PART
+            for table in range(2):
+                for d in range(3):
+                    y_send[LAST, d, table, PART + i] = early_recv[k, table, (y + d + 1) % 4, t]
+                own[LAST, table, PART + i] = early_recv[k, table, y, t]
+            return carry
+
+        lax.fori_loop(0, 3 * PART, body, 0)
+
+    prepare(0)
+    pl.semaphore_wait(barrier, 9)
+    send(0)
+    tokens(0)
+    lax.fori_loop(1, 2, ahead, 0)
+    prepare_early()
+    lax.fori_loop(2, LAST, ahead, 0)
+    await_tokens(0)
+    tokens(1)
+    prepare_last()
+    send(LAST)
 
     sums_ref[...] = jnp.zeros_like(sums_ref)
 
@@ -215,9 +285,10 @@
         def body(i, sums):
             part, t = i // PART, i % PART
             tile = (x + part) % 4 * PART + t
+            is_last = step // LAST
+            tile = tile + (i - tile) * is_last
             tables = [
-                [raw_value(step, table, y * TILES + tile)]
-                + [decode(y_recv[step, k, table, tile]) for k in (1, 0, 2)]
+                [decode(own[step, table, tile])] + [decode(y_recv[step, k, table, tile]) for k in (1, 0, 2)]
                 for table in range(2)
             ]
             select, proof, sums = two_rounds(tables[0], tables[1], sums, y_scalars)
@@ -233,24 +304,25 @@
             return carry
 
         lax.fori_loop(0, 3 * PART, coded, 0)
-        for k in range(3):
-            x_copy(step, k).start()
+
+        @pl.when(step < LAST)
+        def _():
+            for k in range(3):
+                x_copy(step, k).start()
+
         for t in range(PART):
             for table in range(2):
                 x_own[table, TILES + step * PART + t] = x_own[table, t]
 
-    def x_phase(step):
-        for k in range(3):
-            x_copy(step, k).wait_recv()
-
+    def x_phase(step, received):
         def body(t, sums):
             tables = [
-                [x_own[table, TILES + step * PART + t]] + [decode(x_recv[step, k, table, t]) for k in (1, 0, 2)]
+                [x_own[table, TILES + step * PART + t]] + [decode(received[step, k, table, t]) for k in (1, 0, 2)]
                 for table in range(2)
             ]
             select, proof, sums = two_rounds(tables[0], tables[1], sums, x_scalars)
-            for table, value in ((0, select), (1, proof)):
-                done[table, step, t] = jnp.where(value == MODULUS, 0, value)
+            for ref, value in ((out_selects, select), (out_proofs, proof)):
+                ref[step, t] = jnp.where(value == MODULUS, 0, value)
             return sums
 
         store_sums(1, lax.fori_loop(0, PART, body, load_sums(1)))
@@ -260,18 +332,14 @@
 
         @pl.when(step >= 1)
         def _():
-            x_phase(step - 1)
+            for k in range(3):
+                x_copy(step - 1, k).wait_recv()
+            x_phase(step - 1, x_recv)
 
         return carry
 
     lax.fori_loop(0, STEPS, main, 0)
-    x_phase(STEPS - 1)
-
-    outs = [
-        pltpu.make_async_copy(done.at[table], (out_selects, out_proofs)[table], out_sem.at[table]) for table in range(2)
-    ]
-    for copy in outs:
-        copy.start()
+    x_phase(LAST, x_send)
 
     row = lax.broadcasted_iota(I32, (8, 128), 0)
     lane = lax.broadcasted_iota(I32, (8, 128), 1)
@@ -323,6 +391,7 @@
         plane_copy(m).wait_recv()
         total = total + gathered[m]
     tile_out[1] = total
+    await_tokens(1)
     for m in range(1, 8):
         z_copy(m).start()
     for m in range(1, 8):
@@ -342,73 +411,81 @@
     for limb, piece in enumerate((value & 2047, srl(value, 11) & 2047, srl(value, 22))):
         out_points[limb] = piece.astype(F32)[:4, :3]
 
-    for copy in outs:
-        copy.wait()
-
     def finish(step, carry):
         for k in range(3):
             y_copy(step, k).wait_send()
             x_copy(step, k).wait_send()
         return carry
 
-    lax.fori_loop(0, STEPS, finish, 0)
+    lax.fori_loop(0, LAST, finish, 0)
+    for k in range(3):
+        y_copy(LAST, k).wait_send()
+        early_copy(k).wait_send()
     for m in range(1, 16):
         plane_copy(m).wait_send()
     for m in range(1, 8):
         z_copy(m).wait_send()
 
 
+def write(points, selects, proofs, out_points, out_selects, out_proofs):
+    out_points[...] = points[...]
+    for ints, out in ((selects, out_selects), (proofs, out_proofs)):
+        v = ints[...]
+        for limb, piece in enumerate((v & 2047, srl(v, 11) & 2047, srl(v, 22))):
+            out[limb] = piece.astype(F32)
+
+
 def shards(selectors, proofs, challenges):
-    points, selects, proofs_done = pl.pallas_call(
+    vmem = pl.BlockSpec(memory_space=pltpu.VMEM)
+    ints = jax.ShapeDtypeStruct((STEPS, PART, 8, 128), I32)
+    results = pl.pallas_call(
         kernel,
-        out_shape=(
-            jax.ShapeDtypeStruct((3, 4, 3), F32),
-            jax.ShapeDtypeStruct((STEPS, PART, 8, 128), I32),
-            jax.ShapeDtypeStruct((STEPS, PART, 8, 128), I32),
-        ),
+        out_shape=(jax.ShapeDtypeStruct((3, 4, 3), F32), ints, ints),
         in_specs=[
             pl.BlockSpec(memory_space=pltpu.SMEM),
             pl.BlockSpec(memory_space=pltpu.HBM),
             pl.BlockSpec(memory_space=pltpu.HBM),
         ],
-        out_specs=(
-            pl.BlockSpec(memory_space=pltpu.VMEM),
-            pl.BlockSpec(memory_space=pltpu.HBM),
-            pl.BlockSpec(memory_space=pltpu.HBM),
-        ),
+        out_specs=(vmem, vmem, vmem),
         scratch_shapes=[
             pltpu.VMEM((STEPS, 2, 3, 64, 8, 128), F32),
+            pltpu.VMEM((STEPS, 2, TILES, 8, 128), F32),
             pltpu.VMEM((STEPS, 3, 2, TILES, 8, 128), F32),
             pltpu.VMEM((STEPS, 3, 2, TILES, 8, 128), F32),
+            pltpu.VMEM((3, 2, 4, PART, 8, 128), F32),
+            pltpu.VMEM((3, 2, 4, PART, 8, 128), F32),
             pltpu.VMEM((2, TILES + STEPS * PART, 8, 128), I32),
             pltpu.VMEM((STEPS, 3, 2, PART, 8, 128), F32),
             pltpu.VMEM((STEPS, 3, 2, PART, 8, 128), F32),
             pltpu.VMEM((2, 8, 2, 8, 128), I32),
-            pltpu.VMEM((2, STEPS, PART, 8, 128), I32),
             pltpu.VMEM((16, 8, 128), F32),
             pltpu.VMEM((8, 8, 128), F32),
             pltpu.VMEM((2, 8, 128), F32),
             pltpu.SemaphoreType.DMA((STEPS, 2)),
             pltpu.SemaphoreType.DMA((STEPS, 3)),
             pltpu.SemaphoreType.DMA((STEPS, 3)),
+            pltpu.SemaphoreType.DMA((3,)),
+            pltpu.SemaphoreType.DMA((3,)),
             pltpu.SemaphoreType.DMA((STEPS, 3)),
             pltpu.SemaphoreType.DMA((STEPS, 3)),
             pltpu.SemaphoreType.DMA((16,)),
             pltpu.SemaphoreType.DMA((16,)),
             pltpu.SemaphoreType.DMA((8,)),
             pltpu.SemaphoreType.DMA((8,)),
-            pltpu.SemaphoreType.DMA((2,)),
+            pltpu.SemaphoreType.REGULAR((2, 3)),
         ],
         compiler_params=pltpu.CompilerParams(collective_id=0, has_side_effects=True, vmem_limit_bytes=60 << 20),
         name="sumcheck",
     )(challenges, selectors.reshape(3, 8, 64, 8, 128), proofs.reshape(3, 8, 64, 8, 128))
-
-    def limbs(values):
-        values = jnp.broadcast_to(values.reshape(1, 8, 32, 128), (3, 8, 32, 128))
-        place = lax.broadcasted_iota(I32, values.shape, 0)
-        return (lax.shift_right_logical(values, 11 * place) & 2047).astype(F32).reshape(3, 8, 1, 1, 4096)
-
-    return points, limbs(selects), limbs(proofs_done)
+    limbs = jax.ShapeDtypeStruct((3, STEPS, PART, 8, 128), F32)
+    points, selects, proofs_done = pl.pallas_call(
+        write,
+        out_shape=(jax.ShapeDtypeStruct((3, 4, 3), F32), limbs, limbs),
+        in_specs=[vmem, vmem, vmem],
+        out_specs=(vmem, vmem, vmem),
+        name="write_limbs",
+    )(*results)
+    return points, selects.reshape(3, 8, 1, 1, 4096), proofs_done.reshape(3, 8, 1, 1, 4096)
 
 
 def solution(mesh):

time: 79.2 us -> 74 us (0.934)
  local copies, waits for them, and re-layouts: 2.41 us -> 0 us
  other arithmetic: 1.73 us -> 0 us
  Pallas kernels: 74.2 us -> 73.2 us
    convert_element_type x1 -> x0, other arithmetic: 1.72 us -> none  [limbs(): (lax.shift_right_logical(values, 11 * place) & 2047).astype(F32)]
    unnamed x1 -> x0, local copies, waits for them, and re-layouts: 1.28 us -> none
    broadcast_in_dim x1 -> x0, local copies, waits for them, and re-layouts: 1.12 us -> none  [limbs(): values = jnp.broadcast_to(values.reshape(1, 8, 32, 128), (3, 8, 32, 128))]
    pallas_call x1 -> x2, Pallas kernels: 74.2 us -> 73.2 us  [the longest x1 71.3 us: shards(): pl.pallas_call(kernel, out_shape=(jax.ShapeDtypeStruct((3, 4, 3), F32), i...]
where the time goes in v2:
time: 74 us; the launch traced here: 73.9 us
  Pallas kernels  73.2 us (99%)
    pallas_call x1, Pallas kernels, shards(): pl.pallas_call(kernel, out_shape=(jax.ShapeDtypeStruct((3, 4, 3), F32), i...  71.3 us
    pallas_call x1, Pallas kernels, shards(): pl.pallas_call(write, out_shape=(jax.ShapeDtypeStruct((3, 4, 3), F32), li...  1.9 us

profile of v2, /device:TPU:1, one launch (start us, length us, event | category | flops | bytes accessed | tf_op | source)
XLA Modules:
  0.0 73.9 jit_solution(18036770768861841505)
XLA Ops:
  0.6 71.3 %sumcheck.1 = (f32[3,4,3]{2,1,0:T(4,128)}, s32[8,4,8,128]{3,2,1,0:T(8,128)}, s32[8,4,8,128]{3,2,1,0:T(8,128)}) custom-call(s32[4]{0:T(128)} %challenges.1, f32[3,8,64,8,128]{4,3,2,1,0:T(8,128)} %bitcast.4, f32[3,8,64,8,128]{4,3,2,1,0:T(8,128)} %bitcast.5), custom_call_target="tpu_custom_call" | custom-call | tf_op jit(solution)/shard_map/sumcheck/pallas_call | solution.py:441
  72.0 1.9 %write_limbs.1 = (f32[3,4,3]{2,1,0:T(4,128)}, f32[3,8,4,8,128]{4,3,2,1,0:T(8,128)}, f32[3,8,4,8,128]{4,3,2,1,0:T(8,128)}) custom-call(f32[3,4,3]{2,1,0:T(4,128)} %get-tuple-element.9.points, s32[8,4,8,128]{3,2,1,0:T(8,128)} %get-tuple-element.10.selects, s32[8,4,8,128]{3,2,1,0:T(8,128)} %get-tuple-element.11.proofs), custom_call_target="tpu_custom_call" | custom-call | tf_op jit(solution)/shard_map/write_limbs/pallas_call | solution.py:481

commit v3 on v2

--- a/solution.py
+++ b/solution.py
@@ -13,6 +13,7 @@
 LAST = STEPS - 1
 TILES = 16
 PART = 4
+FAR_FIRST = (10, 9, 11, 6, 14, 5, 7, 13, 15, 2, 8, 1, 3, 4, 12)
 NEAR = (1, 3, 4)
 
 
@@ -113,10 +114,10 @@
 
 
 def kernel(
-    challenges, selectors, proofs, out_points, out_selects, out_proofs,
-    raw, own, y_send, y_recv, early_send, early_recv, x_own, x_send, x_recv, sums_ref, gathered, gathered_z, tile_out,
+    challenges_in, selectors, proofs, out_points, out_selects, out_proofs,
+    raw, own, y_send, y_recv, early_send, early_recv, x_own, x_send, x_recv, sums_ref, gathered, gathered_z, tile_out, challenges,
     raw_sem, y_send_sem, y_recv_sem, early_send_sem, early_recv_sem, x_send_sem, x_recv_sem,
-    plane_send_sem, plane_recv_sem, z_send_sem, z_recv_sem, token_sem,
+    last_send_sem, last_recv_sem, plane_send_sem, plane_recv_sem, z_send_sem, z_recv_sem, token_sem, challenge_sem,
 ):
     gx, gy = lax.axis_index("gx"), lax.axis_index("gy")
     y, z_low = gx // 2, gx % 2
@@ -142,6 +143,13 @@
             device_id=plane_peer(k + 1, 0), device_id_type=MESH,
         )
 
+    def last_copy(t, k):
+        return pltpu.make_async_remote_copy(
+            y_send.at[LAST, k, :, pl.ds(4 * t, 4)], y_recv.at[LAST, k, :, pl.ds(4 * t, 4)],
+            last_send_sem.at[t, k], last_recv_sem.at[t, k],
+            device_id=plane_peer(k + 1, 0), device_id_type=MESH,
+        )
+
     def x_copy(step, k):
         return pltpu.make_async_remote_copy(
             x_send.at[step, k], x_recv.at[step, k], x_send_sem.at[step, k], x_recv_sem.at[step, k],
@@ -171,6 +179,8 @@
     for step in range(STEPS):
         for table in range(2):
             load(step, table).start()
+    challenge_copy = pltpu.make_async_copy(challenges_in, challenges, challenge_sem)
+    challenge_copy.start()
 
     def raw_value(step, table, tile):
         low, middle, high = (raw[step, table, limb, tile].astype(I32) for limb in range(3))
@@ -223,13 +233,13 @@
         def mine(i, carry):
             k, t = i // PART, i % PART
             for table in range(2):
-                y_send[LAST, k, table, t] = encode(raw_value(LAST, table, (y + k + 1) % 4 * TILES + x * PART + t))
+                y_send[LAST, k, table, 4 * t] = encode(raw_value(LAST, table, (y + k + 1) % 4 * TILES + x * PART + t))
             return carry
 
         lax.fori_loop(0, 3 * PART, mine, 0)
         for t in range(PART):
             for table in range(2):
-                own[LAST, table, t] = encode(raw_value(LAST, table, y * TILES + x * PART + t))
+                own[LAST, table, 4 * t] = encode(raw_value(LAST, table, y * TILES + x * PART + t))
 
     def prepare_last():
         for k in range(3):
@@ -239,8 +249,8 @@
             k, t = i // PART, i % PART
             for table in range(2):
                 for d in range(3):
-                    y_send[LAST, d, table, PART + i] = early_recv[k, table, (y + d + 1) % 4, t]
-                own[LAST, table, PART + i] = early_recv[k, table, y, t]
+                    y_send[LAST, d, table, 4 * t + k + 1] = early_recv[k, table, (y + d + 1) % 4, t]
+                own[LAST, table, 4 * t + k + 1] = early_recv[k, table, y, t]
             return carry
 
         lax.fori_loop(0, 3 * PART, body, 0)
@@ -255,7 +265,9 @@
     await_tokens(0)
     tokens(1)
     prepare_last()
-    send(LAST)
+    for t in range(PART):
+        for k in range(3):
+            last_copy(t, k).start()
 
     sums_ref[...] = jnp.zeros_like(sums_ref)
 
@@ -275,6 +287,7 @@
             for part in range(2):
                 sums_ref[phase, i, part] = sums[i][part]
 
+    challenge_copy.wait()
     y_scalars = phase_scalars(y, 0, 1)
     x_scalars = phase_scalars(x, 2, 3)
 
@@ -285,8 +298,6 @@
         def body(i, sums):
             part, t = i // PART, i % PART
             tile = (x + part) % 4 * PART + t
-            is_last = step // LAST
-            tile = tile + (i - tile) * is_last
             tables = [
                 [decode(own[step, table, tile])] + [decode(y_recv[step, k, table, tile]) for k in (1, 0, 2)]
                 for table in range(2)
@@ -305,41 +316,70 @@
 
         lax.fori_loop(0, 3 * PART, coded, 0)
 
-        @pl.when(step < LAST)
-        def _():
-            for k in range(3):
-                x_copy(step, k).start()
-
+        for k in range(3):
+            x_copy(step, k).start()
         for t in range(PART):
             for table in range(2):
                 x_own[table, TILES + step * PART + t] = x_own[table, t]
 
-    def x_phase(step, received):
+    def finished(step, t, select, proof):
+        for ref, value in ((out_selects, select), (out_proofs, proof)):
+            ref[step, t] = jnp.where(value == MODULUS, 0, value)
+
+    def x_phase(step):
+        for k in range(3):
+            x_copy(step, k).wait_recv()
+
         def body(t, sums):
             tables = [
-                [x_own[table, TILES + step * PART + t]] + [decode(received[step, k, table, t]) for k in (1, 0, 2)]
+                [x_own[table, TILES + step * PART + t]] + [decode(x_recv[step, k, table, t]) for k in (1, 0, 2)]
                 for table in range(2)
             ]
             select, proof, sums = two_rounds(tables[0], tables[1], sums, x_scalars)
-            for ref, value in ((out_selects, select), (out_proofs, proof)):
-                ref[step, t] = jnp.where(value == MODULUS, 0, value)
+            finished(step, t, select, proof)
             return sums
 
         store_sums(1, lax.fori_loop(0, PART, body, load_sums(1)))
+
+    def last_phase(t):
+        for k in range(3):
+            last_copy(t, k).wait_recv()
+
+        def body(r, sums):
+            tables = [
+                [decode(own[LAST, table, 4 * t + r])] + [decode(y_recv[LAST, k, table, 4 * t + r]) for k in (1, 0, 2)]
+                for table in range(2)
+            ]
+            x_own[0, r], x_own[1, r], sums = two_rounds(tables[0], tables[1], sums, y_scalars)
+            return sums
+
+        store_sums(0, lax.fori_loop(0, 4, body, load_sums(0)))
+        tables = [[x_own[table, r] for r in (0, 2, 1, 3)] for table in range(2)]
+        select, proof, sums = two_rounds(tables[0], tables[1], load_sums(1), x_scalars)
+        store_sums(1, sums)
+        finished(LAST, t, select, proof)
 
     def main(step, carry):
         y_phase(step)
 
         @pl.when(step >= 1)
         def _():
-            for k in range(3):
-                x_copy(step - 1, k).wait_recv()
-            x_phase(step - 1, x_recv)
+            x_phase(step - 1)
 
         return carry
 
-    lax.fori_loop(0, STEPS, main, 0)
-    x_phase(LAST, x_send)
+    lax.fori_loop(0, LAST, main, 0)
+
+    def last(t, carry):
+        last_phase(t)
+
+        @pl.when(t == 2)
+        def _():
+            x_phase(LAST - 1)
+
+        return carry
+
+    lax.fori_loop(0, PART, last, 0)
 
     row = lax.broadcasted_iota(I32, (8, 128), 0)
     lane = lax.broadcasted_iota(I32, (8, 128), 1)
@@ -374,29 +414,43 @@
 
     def plane_copy(m):
         return pltpu.make_async_remote_copy(
-            tile_out.at[0], gathered.at[m], plane_send_sem.at[m], plane_recv_sem.at[m],
+            tile_out.at[1], gathered.at[m], plane_send_sem.at[m], plane_recv_sem.at[m],
             device_id=plane_peer(m // 4, m % 4), device_id_type=MESH,
         )
 
     def z_copy(m):
         return pltpu.make_async_remote_copy(
-            tile_out.at[1], gathered_z.at[m], z_send_sem.at[m], z_recv_sem.at[m],
+            tile_out.at[0], gathered_z.at[m], z_send_sem.at[m], z_recv_sem.at[m],
             device_id=z_peer(m), device_id_type=MESH,
         )
 
-    for m in range(1, 16):
+    await_tokens(1)
+    for m in range(1, 8):
+        z_copy(m).start()
+
+    def finish(step, carry):
+        for k in range(3):
+            y_copy(step, k).wait_send()
+            x_copy(step, k).wait_send()
+        return carry
+
+    lax.fori_loop(0, LAST, finish, 0)
+    for k in range(3):
+        early_copy(k).wait_send()
+        for t in range(PART):
+            last_copy(t, k).wait_send()
+    total = tile_out[0]
+    for m in range(1, 8):
+        z_copy(m).wait_recv()
+        total = total + gathered_z[m]
+    tile_out[1] = total
+    for m in FAR_FIRST:
         plane_copy(m).start()
-    total = tile_out[0]
+    for m in range(1, 8):
+        z_copy(m).wait_send()
     for m in range(1, 16):
         plane_copy(m).wait_recv()
         total = total + gathered[m]
-    tile_out[1] = total
-    await_tokens(1)
-    for m in range(1, 8):
-        z_copy(m).start()
-    for m in range(1, 8):
-        z_copy(m).wait_recv()
-        total = total + gathered_z[m]
 
     limbs = total.astype(I32)
     middle, high = pltpu.roll(limbs, 125, 1), pltpu.roll(limbs, 122, 1)
@@ -411,20 +465,8 @@
     for limb, piece in enumerate((value & 2047, srl(value, 11) & 2047, srl(value, 22))):
         out_points[limb] = piece.astype(F32)[:4, :3]
 
-    def finish(step, carry):
-        for k in range(3):
-            y_copy(step, k).wait_send()
-            x_copy(step, k).wait_send()
-        return carry
-
-    lax.fori_loop(0, LAST, finish, 0)
-    for k in range(3):
-        y_copy(LAST, k).wait_send()
-        early_copy(k).wait_send()
     for m in range(1, 16):
         plane_copy(m).wait_send()
-    for m in range(1, 8):
-        z_copy(m).wait_send()
 
 
 def write(points, selects, proofs, out_points, out_selects, out_proofs):
@@ -437,12 +479,13 @@
 
 def shards(selectors, proofs, challenges):
     vmem = pl.BlockSpec(memory_space=pltpu.VMEM)
-    ints = jax.ShapeDtypeStruct((STEPS, PART, 8, 128), I32)
+    tables = [t.reshape(3, 8, 64, 8, 128) for t in (selectors, proofs)]
+    ints = pltpu.VMEM((STEPS, PART, 8, 128), I32)
     results = pl.pallas_call(
         kernel,
-        out_shape=(jax.ShapeDtypeStruct((3, 4, 3), F32), ints, ints),
+        out_shape=(pltpu.VMEM((3, 4, 3), F32), ints, ints),
         in_specs=[
-            pl.BlockSpec(memory_space=pltpu.SMEM),
+            pl.BlockSpec(memory_space=pltpu.HBM),
             pl.BlockSpec(memory_space=pltpu.HBM),
             pl.BlockSpec(memory_space=pltpu.HBM),
         ],
@@ -461,6 +504,7 @@
             pltpu.VMEM((16, 8, 128), F32),
             pltpu.VMEM((8, 8, 128), F32),
             pltpu.VMEM((2, 8, 128), F32),
+            pltpu.SMEM((4,), I32),
             pltpu.SemaphoreType.DMA((STEPS, 2)),
             pltpu.SemaphoreType.DMA((STEPS, 3)),
             pltpu.SemaphoreType.DMA((STEPS, 3)),
@@ -468,15 +512,18 @@
             pltpu.SemaphoreType.DMA((3,)),
             pltpu.SemaphoreType.DMA((STEPS, 3)),
             pltpu.SemaphoreType.DMA((STEPS, 3)),
+            pltpu.SemaphoreType.DMA((PART, 3)),
+            pltpu.SemaphoreType.DMA((PART, 3)),
             pltpu.SemaphoreType.DMA((16,)),
             pltpu.SemaphoreType.DMA((16,)),
             pltpu.SemaphoreType.DMA((8,)),
             pltpu.SemaphoreType.DMA((8,)),
             pltpu.SemaphoreType.REGULAR((2, 3)),
+            pltpu.SemaphoreType.DMA,
         ],
-        compiler_params=pltpu.CompilerParams(collective_id=0, has_side_effects=True, vmem_limit_bytes=60 << 20),
+        compiler_params=pltpu.CompilerParams(collective_id=0, has_side_effects=True, vmem_limit_bytes=40 << 20),
         name="sumcheck",
-    )(challenges, selectors.reshape(3, 8, 64, 8, 128), proofs.reshape(3, 8, 64, 8, 128))
+    )(*(pltpu.with_memory_space_constraint(t, pltpu.HBM) for t in (challenges, *tables)))
     limbs = jax.ShapeDtypeStruct((3, STEPS, PART, 8, 128), F32)
     points, selects, proofs_done = pl.pallas_call(
         write,
@@ -484,7 +531,7 @@
         in_specs=[vmem, vmem, vmem],
         out_specs=(vmem, vmem, vmem),
         name="write_limbs",
-    )(*results)
+    )(*(pltpu.with_memory_space_constraint(r, pltpu.VMEM) for r in results))
     return points, selects.reshape(3, 8, 1, 1, 4096), proofs_done.reshape(3, 8, 1, 1, 4096)
 
 

time: 74 us -> 69.4 us (0.938)
  Pallas kernels: 73.2 us -> 68.6 us
    pallas_call x1, Pallas kernels: 71.3 us -> 67.7 us  [shards(): pl.pallas_call(kernel, out_shape=(pltpu.VMEM((3, 4, 3), F32), ints, ints)...]
    pallas_call x1, Pallas kernels: 1.9 us -> 0.91 us  [shards(): pl.pallas_call(write, out_shape=(jax.ShapeDtypeStruct((3, 4, 3), F32), li...]
where the time goes in v3:
time: 69.4 us; the launch traced here: 69.3 us
  Pallas kernels  68.6 us (99%)
    pallas_call x1, Pallas kernels, shards(): pl.pallas_call(kernel, out_shape=(pltpu.VMEM((3, 4, 3), F32), ints, ints)...  67.7 us

profile of v3, /device:TPU:1, one launch (start us, length us, event | category | flops | bytes accessed | tf_op | source)
XLA Modules:
  0.0 69.3 jit_solution(14549587582901110632)
XLA Ops:
  0.6 67.7 %sumcheck.1 = (f32[3,4,3]{2,1,0:T(4,128)S(1)}, s32[8,4,8,128]{3,2,1,0:T(8,128)S(1)}, s32[8,4,8,128]{3,2,1,0:T(8,128)S(1)}) custom-call(s32[4]{0:T(128)} %challenges_in.1, f32[3,8,64,8,128]{4,3,2,1,0:T(8,128)} %bitcast.4, f32[3,8,64,8,128]{4,3,2,1,0:T(8,128)} %bitcast.5), custom_call_target="tpu_custom_call" | custom-call | tf_op jit(solution)/shard_map/sumcheck/pallas_call | solution.py:484
  68.3 0.9 %write_limbs.1 = (f32[3,4,3]{2,1,0:T(4,128)}, f32[3,8,4,8,128]{4,3,2,1,0:T(8,128)}, f32[3,8,4,8,128]{4,3,2,1,0:T(8,128)}) custom-call(f32[3,4,3]{2,1,0:T(4,128)S(1)} %get-tuple-element.9.points, s32[8,4,8,128]{3,2,1,0:T(8,128)S(1)} %get-tuple-element.10.selects, s32[8,4,8,128]{3,2,1,0:T(8,128)S(1)} %get-tuple-element.11.proofs), custom_call_target="tpu_custom_call" | custom-call | tf_op jit(solution)/shard_map/write_limbs/pallas_call | solution.py:528

commit v4 on v3

--- a/solution.py
+++ b/solution.py
@@ -10,7 +10,8 @@
 F32 = jnp.float32
 MODULUS = 0x7FFFFFFF
 STEPS = 8
-LAST = STEPS - 1
+EARLY = 2
+LATE = STEPS - EARLY
 TILES = 16
 PART = 4
 FAR_FIRST = (10, 9, 11, 6, 14, 5, 7, 13, 15, 2, 8, 1, 3, 4, 12)
@@ -143,10 +144,10 @@
             device_id=plane_peer(k + 1, 0), device_id_type=MESH,
         )
 
-    def last_copy(t, k):
+    def last_copy(e, t, k):
         return pltpu.make_async_remote_copy(
-            y_send.at[LAST, k, :, pl.ds(4 * t, 4)], y_recv.at[LAST, k, :, pl.ds(4 * t, 4)],
-            last_send_sem.at[t, k], last_recv_sem.at[t, k],
+            y_send.at[LATE + e, k, :, pl.ds(4 * t, 4)], y_recv.at[LATE + e, k, :, pl.ds(4 * t, 4)],
+            last_send_sem.at[e, t, k], last_recv_sem.at[e, t, k],
             device_id=plane_peer(k + 1, 0), device_id_type=MESH,
         )
 
@@ -156,11 +157,14 @@
             device_id=plane_peer(0, k + 1), device_id_type=MESH,
         )
 
-    def early_copy(k):
+    def early_copy(e, k):
         return pltpu.make_async_remote_copy(
-            early_send.at[k], early_recv.at[k], early_send_sem.at[k], early_recv_sem.at[k],
+            early_send.at[e, k], early_recv.at[e, k], early_send_sem.at[e, k], early_recv_sem.at[e, k],
             device_id=plane_peer(0, k + 1), device_id_type=MESH,
         )
+
+    gathered[...] = jnp.zeros_like(gathered)
+    gathered_z[...] = jnp.zeros_like(gathered_z)
 
     barrier = pltpu.get_barrier_semaphore()
     for m in range(1, 4):
@@ -215,59 +219,63 @@
         send(step)
         return carry
 
-    def prepare_early():
+    def prepare_early(e, outer):
+        step = LATE + e
         for table in range(2):
-            load(LAST, table).wait()
+            load(step, table).wait()
 
         def body(i, carry):
             k, quarter, t = i // TILES, i % TILES // PART, i % PART
             tile = quarter * TILES + (x + k + 1) % 4 * PART + t
             for table in range(2):
-                early_send[k, table, quarter, t] = encode(raw_value(LAST, table, tile))
+                early_send[e, k, table, quarter, t] = encode(raw_value(step, table, tile))
             return carry
 
         lax.fori_loop(0, 3 * TILES, body, 0)
         for k in range(3):
-            early_copy(k).start()
+            early_copy(e, k).start()
 
         def mine(i, carry):
             k, t = i // PART, i % PART
             for table in range(2):
-                y_send[LAST, k, table, 4 * t] = encode(raw_value(LAST, table, (y + k + 1) % 4 * TILES + x * PART + t))
+                y_send[step, k, table, 4 * t] = encode(raw_value(step, table, (y + k + 1) % 4 * TILES + x * PART + t))
             return carry
 
         lax.fori_loop(0, 3 * PART, mine, 0)
         for t in range(PART):
             for table in range(2):
-                own[LAST, table, 4 * t] = encode(raw_value(LAST, table, y * TILES + x * PART + t))
-
-    def prepare_last():
-        for k in range(3):
-            early_copy(k).wait_recv()
+                own[step, table, 4 * t] = encode(raw_value(step, table, y * TILES + x * PART + t))
+        return outer
+
+    def prepare_last(e, outer):
+        step = LATE + e
+        for k in range(3):
+            early_copy(e, k).wait_recv()
 
         def body(i, carry):
             k, t = i // PART, i % PART
             for table in range(2):
                 for d in range(3):
-                    y_send[LAST, d, table, 4 * t + k + 1] = early_recv[k, table, (y + d + 1) % 4, t]
-                own[LAST, table, 4 * t + k + 1] = early_recv[k, table, y, t]
+                    y_send[step, d, table, 4 * t + k + 1] = early_recv[e, k, table, (y + d + 1) % 4, t]
+                own[step, table, 4 * t + k + 1] = early_recv[e, k, table, y, t]
             return carry
 
         lax.fori_loop(0, 3 * PART, body, 0)
+        for t in range(PART):
+            for k in range(3):
+                last_copy(e, t, k).start()
+        return outer
 
     prepare(0)
     pl.semaphore_wait(barrier, 9)
     send(0)
     tokens(0)
     lax.fori_loop(1, 2, ahead, 0)
-    prepare_early()
-    lax.fori_loop(2, LAST, ahead, 0)
+    lax.fori_loop(0, EARLY, prepare_early, 0)
+    lax.fori_loop(2, LATE, ahead, 0)
     await_tokens(0)
     tokens(1)
-    prepare_last()
-    for t in range(PART):
-        for k in range(3):
-            last_copy(t, k).start()
+    lax.fori_loop(0, EARLY, prepare_last, 0)
 
     sums_ref[...] = jnp.zeros_like(sums_ref)
 
@@ -341,13 +349,14 @@
 
         store_sums(1, lax.fori_loop(0, PART, body, load_sums(1)))
 
-    def last_phase(t):
-        for k in range(3):
-            last_copy(t, k).wait_recv()
+    def last_phase(e, t):
+        step = LATE + e
+        for k in range(3):
+            last_copy(e, t, k).wait_recv()
 
         def body(r, sums):
             tables = [
-                [decode(own[LAST, table, 4 * t + r])] + [decode(y_recv[LAST, k, table, 4 * t + r]) for k in (1, 0, 2)]
+                [decode(own[step, table, 4 * t + r])] + [decode(y_recv[step, k, table, 4 * t + r]) for k in (1, 0, 2)]
                 for table in range(2)
             ]
             x_own[0, r], x_own[1, r], sums = two_rounds(tables[0], tables[1], sums, y_scalars)
@@ -357,7 +366,7 @@
         tables = [[x_own[table, r] for r in (0, 2, 1, 3)] for table in range(2)]
         select, proof, sums = two_rounds(tables[0], tables[1], load_sums(1), x_scalars)
         store_sums(1, sums)
-        finished(LAST, t, select, proof)
+        finished(step, t, select, proof)
 
     def main(step, carry):
         y_phase(step)
@@ -368,18 +377,18 @@
 
         return carry
 
-    lax.fori_loop(0, LAST, main, 0)
-
-    def last(t, carry):
-        last_phase(t)
-
-        @pl.when(t == 2)
+    lax.fori_loop(0, LATE, main, 0)
+
+    def last(i, carry):
+        last_phase(i // PART, i % PART)
+
+        @pl.when(i == PART)
         def _():
-            x_phase(LAST - 1)
+            x_phase(LATE - 1)
 
         return carry
 
-    lax.fori_loop(0, PART, last, 0)
+    lax.fori_loop(0, EARLY * PART, last, 0)
 
     row = lax.broadcasted_iota(I32, (8, 128), 0)
     lane = lax.broadcasted_iota(I32, (8, 128), 1)
@@ -414,13 +423,13 @@
 
     def plane_copy(m):
         return pltpu.make_async_remote_copy(
-            tile_out.at[1], gathered.at[m], plane_send_sem.at[m], plane_recv_sem.at[m],
+            tile_out.at[1, :4], gathered.at[m, :4], plane_send_sem.at[m], plane_recv_sem.at[m],
             device_id=plane_peer(m // 4, m % 4), device_id_type=MESH,
         )
 
     def z_copy(m):
         return pltpu.make_async_remote_copy(
-            tile_out.at[0], gathered_z.at[m], z_send_sem.at[m], z_recv_sem.at[m],
+            tile_out.at[0, :4], gathered_z.at[m, :4], z_send_sem.at[m], z_recv_sem.at[m],
             device_id=z_peer(m), device_id_type=MESH,
         )
 
@@ -434,11 +443,16 @@
             x_copy(step, k).wait_send()
         return carry
 
-    lax.fori_loop(0, LAST, finish, 0)
-    for k in range(3):
-        early_copy(k).wait_send()
-        for t in range(PART):
-            last_copy(t, k).wait_send()
+    lax.fori_loop(0, LATE, finish, 0)
+
+    def finish_last(e, carry):
+        for k in range(3):
+            early_copy(e, k).wait_send()
+            for t in range(PART):
+                last_copy(e, t, k).wait_send()
+        return carry
+
+    lax.fori_loop(0, EARLY, finish_last, 0)
     total = tile_out[0]
     for m in range(1, 8):
         z_copy(m).wait_recv()
@@ -495,8 +509,8 @@
             pltpu.VMEM((STEPS, 2, TILES, 8, 128), F32),
             pltpu.VMEM((STEPS, 3, 2, TILES, 8, 128), F32),
             pltpu.VMEM((STEPS, 3, 2, TILES, 8, 128), F32),
-            pltpu.VMEM((3, 2, 4, PART, 8, 128), F32),
-            pltpu.VMEM((3, 2, 4, PART, 8, 128), F32),
+            pltpu.VMEM((EARLY, 3, 2, 4, PART, 8, 128), F32),
+            pltpu.VMEM((EARLY, 3, 2, 4, PART, 8, 128), F32),
             pltpu.VMEM((2, TILES + STEPS * PART, 8, 128), I32),
             pltpu.VMEM((STEPS, 3, 2, PART, 8, 128), F32),
             pltpu.VMEM((STEPS, 3, 2, PART, 8, 128), F32),
@@ -508,12 +522,12 @@
             pltpu.SemaphoreType.DMA((STEPS, 2)),
             pltpu.SemaphoreType.DMA((STEPS, 3)),
             pltpu.SemaphoreType.DMA((STEPS, 3)),
-            pltpu.SemaphoreType.DMA((3,)),
-            pltpu.SemaphoreType.DMA((3,)),
+            pltpu.SemaphoreType.DMA((EARLY, 3)),
+            pltpu.SemaphoreType.DMA((EARLY, 3)),
             pltpu.SemaphoreType.DMA((STEPS, 3)),
             pltpu.SemaphoreType.DMA((STEPS, 3)),
-            pltpu.SemaphoreType.DMA((PART, 3)),
-            pltpu.SemaphoreType.DMA((PART, 3)),
+            pltpu.SemaphoreType.DMA((EARLY, PART, 3)),
+            pltpu.SemaphoreType.DMA((EARLY, PART, 3)),
             pltpu.SemaphoreType.DMA((16,)),
             pltpu.SemaphoreType.DMA((16,)),
             pltpu.SemaphoreType.DMA((8,)),

time: 69.4 us -> 68.5 us (0.987)
  Pallas kernels: 68.6 us -> 67.7 us
    pallas_call x1, Pallas kernels: 67.7 us -> 66.8 us  [shards(): pl.pallas_call(kernel, out_shape=(pltpu.VMEM((3, 4, 3), F32), ints, ints)...]
where the time goes in v4:
time: 68.5 us; the launch traced here: 68.4 us
  Pallas kernels  67.7 us (99%)
    pallas_call x1, Pallas kernels, shards(): pl.pallas_call(kernel, out_shape=(pltpu.VMEM((3, 4, 3), F32), ints, ints)...  66.8 us

profile of v4, /device:TPU:1, one launch (start us, length us, event | category | flops | bytes accessed | tf_op | source)
XLA Modules:
  0.0 68.4 jit_solution(12387561859968209584)
XLA Ops:
  0.6 66.8 %sumcheck.1 = (f32[3,4,3]{2,1,0:T(4,128)S(1)}, s32[8,4,8,128]{3,2,1,0:T(8,128)S(1)}, s32[8,4,8,128]{3,2,1,0:T(8,128)S(1)}) custom-call(s32[4]{0:T(128)} %challenges_in.1, f32[3,8,64,8,128]{4,3,2,1,0:T(8,128)} %bitcast.4, f32[3,8,64,8,128]{4,3,2,1,0:T(8,128)} %bitcast.5), custom_call_target="tpu_custom_call" | custom-call | tf_op jit(solution)/shard_map/sumcheck/pallas_call | solution.py:498
  67.5 0.9 %write_limbs.1 = (f32[3,4,3]{2,1,0:T(4,128)}, f32[3,8,4,8,128]{4,3,2,1,0:T(8,128)}, f32[3,8,4,8,128]{4,3,2,1,0:T(8,128)}) custom-call(f32[3,4,3]{2,1,0:T(4,128)S(1)} %get-tuple-element.9.points, s32[8,4,8,128]{3,2,1,0:T(8,128)S(1)} %get-tuple-element.10.selects, s32[8,4,8,128]{3,2,1,0:T(8,128)S(1)} %get-tuple-element.11.proofs), custom_call_target="tpu_custom_call" | custom-call | tf_op jit(solution)/shard_map/write_limbs/pallas_call | solution.py:542

commit v5 on v4

--- a/solution.py
+++ b/solution.py
@@ -180,7 +180,7 @@
         for m in range(3):
             pl.semaphore_wait(token_sem.at[turn, m], 1)
 
-    for step in range(STEPS):
+    for step in (0, 1, *range(LATE, STEPS), *range(2, LATE)):
         for table in range(2):
             load(step, table).start()
     challenge_copy = pltpu.make_async_copy(challenges_in, challenges, challenge_sem)
@@ -362,7 +362,10 @@
             x_own[0, r], x_own[1, r], sums = two_rounds(tables[0], tables[1], sums, y_scalars)
             return sums
 
-        store_sums(0, lax.fori_loop(0, 4, body, load_sums(0)))
+        sums = load_sums(0)
+        for r in range(4):
+            sums = body(r, sums)
+        store_sums(0, sums)
         tables = [[x_own[table, r] for r in (0, 2, 1, 3)] for table in range(2)]
         select, proof, sums = two_rounds(tables[0], tables[1], load_sums(1), x_scalars)
         store_sums(1, sums)

time: 68.5 us -> 68.4 us (level)
  no operation moved by 1% of the time
where the time goes in v5:
time: 68.4 us; the launch traced here: 68.3 us
  Pallas kernels  67.7 us (99%)
    pallas_call x1, Pallas kernels, shards(): pl.pallas_call(kernel, out_shape=(pltpu.VMEM((3, 4, 3), F32), ints, ints)...  66.8 us

profile of v5, /device:TPU:1, one launch (start us, length us, event | category | flops | bytes accessed | tf_op | source)
XLA Modules:
  0.0 68.3 jit_solution(593400279742226821)
XLA Ops:
  0.6 66.8 %sumcheck.1 = (f32[3,4,3]{2,1,0:T(4,128)S(1)}, s32[8,4,8,128]{3,2,1,0:T(8,128)S(1)}, s32[8,4,8,128]{3,2,1,0:T(8,128)S(1)}) custom-call(s32[4]{0:T(128)} %challenges_in.1, f32[3,8,64,8,128]{4,3,2,1,0:T(8,128)} %bitcast.4, f32[3,8,64,8,128]{4,3,2,1,0:T(8,128)} %bitcast.5), custom_call_target="tpu_custom_call" | custom-call | tf_op jit(solution)/shard_map/sumcheck/pallas_call | solution.py:501
  67.4 0.9 %write_limbs.1 = (f32[3,4,3]{2,1,0:T(4,128)}, f32[3,8,4,8,128]{4,3,2,1,0:T(8,128)}, f32[3,8,4,8,128]{4,3,2,1,0:T(8,128)}) custom-call(f32[3,4,3]{2,1,0:T(4,128)S(1)} %get-tuple-element.9.points, s32[8,4,8,128]{3,2,1,0:T(8,128)S(1)} %get-tuple-element.10.selects, s32[8,4,8,128]{3,2,1,0:T(8,128)S(1)} %get-tuple-element.11.proofs), custom_call_target="tpu_custom_call" | custom-call | tf_op jit(solution)/shard_map/write_limbs/pallas_call | solution.py:545

commit v6 on v5

--- a/solution.py
+++ b/solution.py
@@ -125,13 +125,13 @@
     x, z_core = gy // 4, gy % 4
 
     def plane_peer(dy, dx):
-        return {"gx": (y + dy) % 4 * 2 + z_low, "gy": (x + dx) % 4 * 4 + z_core}
+        return {"gx": lax.rem(y + dy, 4) * 2 + z_low, "gy": lax.rem(x + dx, 4) * 4 + z_core}
 
     def z_peer(m):
         z_high, core = z_core // 2, z_core % 2
         return {
-            "gx": y * 2 + (z_low + m % 2) % 2,
-            "gy": x * 4 + (z_high + m // 2 % 2) % 2 * 2 + (core + m // 4) % 2,
+            "gx": y * 2 + lax.rem(z_low + m % 2, 2),
+            "gy": x * 4 + lax.rem(z_high + m // 2 % 2, 2) * 2 + lax.rem(core + m // 4, 2),
         }
 
     def load(step, table):
@@ -195,8 +195,8 @@
             load(step, table).wait()
 
         def body(i, carry):
-            k, t = i // TILES, i % TILES
-            tile = (y + k + 1) % 4 * TILES + t
+            k, t = lax.div(i, TILES), lax.rem(i, TILES)
+            tile = lax.rem(y + k + 1, 4) * TILES + t
             for table in range(2):
                 y_send[step, k, table, t] = encode(raw_value(step, table, tile))
             return carry
@@ -236,7 +236,7 @@
             early_copy(e, k).start()
 
         def mine(i, carry):
-            k, t = i // PART, i % PART
+            k, t = lax.div(i, PART), lax.rem(i, PART)
             for table in range(2):
                 y_send[step, k, table, 4 * t] = encode(raw_value(step, table, (y + k + 1) % 4 * TILES + x * PART + t))
             return carry
@@ -253,7 +253,7 @@
             early_copy(e, k).wait_recv()
 
         def body(i, carry):
-            k, t = i // PART, i % PART
+            k, t = lax.div(i, PART), lax.rem(i, PART)
             for table in range(2):
                 for d in range(3):
                     y_send[step, d, table, 4 * t + k + 1] = early_recv[e, k, table, (y + d + 1) % 4, t]
@@ -304,8 +304,8 @@
             y_copy(step, k).wait_recv()
 
         def body(i, sums):
-            part, t = i // PART, i % PART
-            tile = (x + part) % 4 * PART + t
+            part, t = lax.div(i, PART), lax.rem(i, PART)
+            tile = lax.rem(x + part, 4) * PART + t
             tables = [
                 [decode(own[step, table, tile])] + [decode(y_recv[step, k, table, tile]) for k in (1, 0, 2)]
                 for table in range(2)
@@ -317,7 +317,7 @@
         store_sums(0, lax.fori_loop(0, TILES, body, load_sums(0)))
 
         def coded(i, carry):
-            k, t = i // PART, i % PART
+            k, t = lax.div(i, PART), lax.rem(i, PART)
             for table in range(2):
                 x_send[step, k, table, t] = encode(x_own[table, PART + i])
             return carry

time: 68.4 us -> 68.2 us (level)
  no operation moved by 1% of the time
where the time goes in v6:
time: 68.2 us; the launch traced here: 68.1 us
  Pallas kernels  67.4 us (99%)
    pallas_call x1, Pallas kernels, shards(): pl.pallas_call(kernel, out_shape=(pltpu.VMEM((3, 4, 3), F32), ints, ints)...  66.5 us

profile of v6, /device:TPU:1, one launch (start us, length us, event | category | flops | bytes accessed | tf_op | source)
XLA Modules:
  0.0 68.1 jit_solution(4968760808705257696)
XLA Ops:
  0.6 66.5 %sumcheck.1 = (f32[3,4,3]{2,1,0:T(4,128)S(1)}, s32[8,4,8,128]{3,2,1,0:T(8,128)S(1)}, s32[8,4,8,128]{3,2,1,0:T(8,128)S(1)}) custom-call(s32[4]{0:T(128)} %challenges_in.1, f32[3,8,64,8,128]{4,3,2,1,0:T(8,128)} %bitcast.4, f32[3,8,64,8,128]{4,3,2,1,0:T(8,128)} %bitcast.5), custom_call_target="tpu_custom_call" | custom-call | tf_op jit(solution)/shard_map/sumcheck/pallas_call | solution.py:501
  67.2 0.9 %write_limbs.1 = (f32[3,4,3]{2,1,0:T(4,128)}, f32[3,8,4,8,128]{4,3,2,1,0:T(8,128)}, f32[3,8,4,8,128]{4,3,2,1,0:T(8,128)}) custom-call(f32[3,4,3]{2,1,0:T(4,128)S(1)} %get-tuple-element.9.points, s32[8,4,8,128]{3,2,1,0:T(8,128)S(1)} %get-tuple-element.10.selects, s32[8,4,8,128]{3,2,1,0:T(8,128)S(1)} %get-tuple-element.11.proofs), custom_call_target="tpu_custom_call" | custom-call | tf_op jit(solution)/shard_map/write_limbs/pallas_call | solution.py:545
